TPU v7x, 128 devices: a whole 4x4x4 slice. The times are simulated.
128 devices in a mesh: tm: 8 (over y, x_hi), nrn: 16 (over x_lo, z, core).
Axes of the slice: x: 4 (x_hi: 2, x_lo: 2; x = x_hi * 2 + x_lo), y: 4, z: 4, core: 2. Of those that a mesh axis runs over, the one named last changes fastest.
Arguments:
- spikes: bfloat16 [32768, 32768], P('tm', 'nrn'), may hold values from -6 to 6
- read_in: bfloat16 [32768, 128], P('nrn'), may hold values from -0.03125 to 0.03125
- kernel: float32 [128, 32768], P(('tm', 'nrn')), may hold values from -0.03125 to 0.03125
- gain: float32 [128], replicated, may hold values from 0.1 to 1.9
- w_gate: bfloat16 [128, 512], replicated, may hold values from -0.5 to 0.5
- w_up: bfloat16 [128, 512], replicated, may hold values from -0.5 to 0.5
- w_down: bfloat16 [512, 128], replicated, may hold values from -0.25 to 0.25
Outputs:
- denoised: bfloat16 [32768, 128], P(('tm', 'nrn'))
All inputs are finite; a program needn't handle non-finite values.
Results may differ from a plain program's by a relative error of at most 0.0045.
Values sent between devices are 32-bit elements; how exact they have to be, the bound alone decides.
No kernel may reach another device: no remote copies, remote signals or barrier semaphores. Data moves between devices by JAX's collectives and lax.ppermute only.
A program may use at most 64 MiB of HBM per device.

v0:
```python
import math

import jax
import jax.numpy as jnp
from jax import lax
from jax.sharding import PartitionSpec as P

precise = lax.Precision.HIGHEST


def dft_table(order):
    index = jnp.arange(order, dtype=jnp.int32)
    phase = index[:, None] * index[None, :] % order
    angles = phase.astype(jnp.float32) * (2.0 * math.pi / order)
    return (jnp.cos(angles), jnp.sin(angles))


def twiddle_table(outer, inner):
    outer_index = jnp.arange(outer, dtype=jnp.int32)
    inner_index = jnp.arange(inner, dtype=jnp.int32)
    phase = outer_index[:, None] * inner_index[None, :] % (outer * inner)
    angles = phase.astype(jnp.float32) * (2.0 * math.pi / (outer * inner))
    return (jnp.cos(angles), jnp.sin(angles))


def forward_dft(signal, tables):
    cos_outer, sin_outer, cos_twist, sin_twist, cos_inner, sin_inner = tables
    real_part = jnp.einsum("ar,crs->cas", cos_outer, signal, precision=precise)
    imag_part = -jnp.einsum("ar,crs->cas", sin_outer, signal, precision=precise)
    twist_real = real_part * cos_twist + imag_part * sin_twist
    twist_imag = imag_part * cos_twist - real_part * sin_twist
    spec_real = jnp.einsum("cas,sb->cab", twist_real, cos_inner, precision=precise) + jnp.einsum(
        "cas,sb->cab", twist_imag, sin_inner, precision=precise
    )
    spec_imag = jnp.einsum("cas,sb->cab", twist_imag, cos_inner, precision=precise) - jnp.einsum(
        "cas,sb->cab", twist_real, sin_inner, precision=precise
    )
    return (spec_real, spec_imag)


def inverse_dft(spec_real, spec_imag, tables):
    cos_outer, sin_outer, cos_twist, sin_twist, cos_inner, sin_inner = tables
    back_real = jnp.einsum("cab,bs->cas", spec_real, cos_inner, precision=precise) - jnp.einsum(
        "cab,bs->cas", spec_imag, sin_inner, precision=precise
    )
    back_imag = jnp.einsum("cab,bs->cas", spec_real, sin_inner, precision=precise) + jnp.einsum(
        "cab,bs->cas", spec_imag, cos_inner, precision=precise
    )
    turn_real = back_real * cos_twist - back_imag * sin_twist
    turn_imag = back_real * sin_twist + back_imag * cos_twist
    result = jnp.einsum("ra,cas->crs", cos_outer, turn_real, precision=precise) - jnp.einsum(
        "ra,cas->crs", sin_outer, turn_imag, precision=precise
    )
    return result / (cos_outer.shape[0] * cos_inner.shape[0])


def per_device(spikes, read_in, kernel, gain, w_gate, w_up, w_down):
    time_groups = lax.axis_size("tm")
    neuron_groups = lax.axis_size("nrn")
    devices = time_groups * neuron_groups
    tok_rows = spikes.shape[0] // neuron_groups
    latent_width = read_in.shape[1]
    channels_dev = latent_width // devices
    session = tok_rows * devices
    latent = lax.psum_scatter(
        jnp.dot(spikes, read_in, preferred_element_type=jnp.float32),
        "nrn",
        scatter_dimension=0,
        tiled=True,
    )
    flipped = latent.T
    series = lax.all_to_all(flipped, ("tm", "nrn"), split_axis=0, concat_axis=1, tiled=True)
    cos_outer, sin_outer = dft_table(devices)
    cos_inner, sin_inner = dft_table(tok_rows)
    cos_twist, sin_twist = twiddle_table(devices, tok_rows)
    tables = (cos_outer, sin_outer, cos_twist, sin_twist, cos_inner, sin_inner)
    data_real, data_imag = forward_dft(series.reshape(channels_dev, devices, tok_rows), tables)
    kern_real, kern_imag = forward_dft(kernel.reshape(channels_dev, devices, tok_rows), tables)
    prod_real = data_real * kern_real - data_imag * kern_imag
    prod_imag = data_real * kern_imag + data_imag * kern_real
    conv = inverse_dft(prod_real, prod_imag, tables).reshape(channels_dev, session)
    mixed = series + conv
    stacked = lax.all_to_all(mixed, ("tm", "nrn"), split_axis=1, concat_axis=0, tiled=True)
    residual = stacked.T
    meansq = jnp.mean(residual * residual, axis=-1, keepdims=True)
    normed = (residual * lax.rsqrt(meansq + 1e-05) * gain).astype(jnp.bfloat16)
    gate = jnp.dot(normed, w_gate, preferred_element_type=jnp.float32)
    upper = jnp.dot(normed, w_up, preferred_element_type=jnp.float32)
    act = (jax.nn.silu(gate) * upper).astype(jnp.bfloat16)
    return (residual + jnp.dot(act, w_down, preferred_element_type=jnp.float32)).astype(
        jnp.bfloat16
    )


def solution(mesh):
    placed = (P("tm", "nrn"), P("nrn", None), P(("tm", "nrn"), None), P(), P(), P(), P())
    return jax.shard_map(
        per_device, mesh=mesh, in_specs=placed, out_specs=P(("tm", "nrn"), None), check_vma=False
    )
```

profile of v0, /device:TPU:1, one launch (start us, length us, event | category | flops | bytes accessed | tf_op | source)
XLA Modules:
  0.0 140.8 jit_solution(16080481978161984792)
XLA Ops:
  6.5 0.0 copy-start
  6.5 0.0 copy-start.1
  6.5 0.0 reduce-scatter.2.cloned.1.call-start
  6.5 1.0 copy-done
  7.6 9.4 %fusion.210 = f32[4096,128]{1,0:T(8,128)} fusion(bf16[4096,2048]{1,0:T(8,128)(2,1)} %param.7, bf16[2048,128]{1,0:T(8,128)(2,1)S(1)} %copy-done), kind=kOutput, calls=%fused_computation.216 | convolution fusion | flops 2147483648 | bytes 19398656 | tf_op jit(solution)/shard_map/dot_general | solution.py:66
  17.0 0.0 copy-start.2
  17.0 0.0 copy-start.3
  17.0 0.0 copy-start.4
  17.0 0.0 copy-start.5
  17.0 0.0 reduce-scatter.2.cloned.1.call-update
  17.1 0.5 broadcast.212
  17.6 0.0 copy-done.1
  17.6 1.0 reduce.3
  18.6 0.6 convolution_bitcast_fusion
  19.1 0.6 fusion.3
  19.7 1.8 %fusion.32 = f32[128,256]{1,0:T(8,128)S(1)} fusion(f32[1,128,256]{1,2,0:T(8,128)S(1)} %convolution_bitcast_fusion, f32[1,128,256]{1,2,0:T(8,128)S(1)} %fusion.3), kind=kOutput, calls=%fused_computation.55 | convolution fusion | flops 102137856 | bytes 393216 | tf_op jit(solution)/shard_map/cas,sb->cab/dot_general | solution.py:35
  21.5 1.8 %fusion.36 = f32[128,256]{1,0:T(8,128)S(1)} fusion(f32[1,128,256]{1,2,0:T(8,128)S(1)} %fusion.3, f32[1,128,256]{1,2,0:T(8,128)S(1)} %convolution_bitcast_fusion), kind=kOutput, calls=%fused_computation.59 | convolution fusion | flops 102137856 | bytes 393216 | tf_op jit(solution)/shard_map/cas,sb->cab/dot_general | solution.py:32
  23.3 1.8 %convolution_subtract_fusion.1 = f32[128,256]{1,0:T(8,128)S(1)} fusion(f32[128,256]{1,0:T(8,128)S(1)} %fusion.32, f32[1,128,256]{1,2,0:T(8,128)S(1)} %fusion.3, f32[1,128,256]{1,2,0:T(8,128)S(1)} %convolution_bitcast_fusion), kind=kOutput, calls=%fused_computation.6 | convolution fusion | flops 102170624 | bytes 524288 | tf_op jit(solution)/shard_map/cas,sb->cab/dot_general | solution.py:35
  25.2 55.0 %reduce-scatter.2.cloned.1.call-done = f32[256,128]{1,0:T(8,128)} async-done(((f32[4096,128]{1,0:T(8,128)}), f32[256,128]{1,0:T(8,128)}) %reduce-scatter.2.cloned.1.call-update) | async-done | bytes 131088 | tf_op jit(solution)/shard_map/reduce_scatter | solution.py:65
  80.1 1.6 %copy.10 = f32[128,1,256]{2,1,0:T(1,128)} copy(f32[128,1,256]{0,2,1:T(8,128)} %bitcast.84) | data formatting | bytes 262144 | tf_op jit(solution)/shard_map/all_to_all | solution.py:72
  81.8 10.8 %all-to-all-start = ((f32[128,1,256]{2,1,0:T(1,128)}), f32[128,1,256]{2,1,0:T(1,128)S(1)}, u32[]{:S(2)}, u32[]{:S(2)}) async-start(f32[128,1,256]{2,1,0:T(1,128)} %copy.10), calls=%async_computation.1 | async-start | bytes 262144 | tf_op jit(solution)/shard_map/all_to_all | solution.py:72
  92.5 1.8 %convolution_add_fusion.1 = f32[128,256]{1,0:T(8,128)S(1)} fusion(f32[128,256]{1,0:T(8,128)S(1)} %fusion.36, f32[1,128,256]{1,2,0:T(8,128)S(1)} %convolution_bitcast_fusion, f32[1,128,256]{1,2,0:T(8,128)S(1)} %fusion.3), kind=kOutput, calls=%fused_computation.8 | convolution fusion | flops 102170624 | bytes 524288 | tf_op jit(solution)/shard_map/cas,sb->cab/dot_general | solution.py:32
  94.4 7.8 %all-to-all-done = f32[128,1,256]{2,1,0:T(1,128)S(1)} async-done(((f32[128,1,256]{2,1,0:T(1,128)}), f32[128,1,256]{2,1,0:T(1,128)S(1)}, u32[]{:S(2)}, u32[]{:S(2)}) %all-to-all-start) | async-done | bytes 131104 | tf_op jit(solution)/shard_map/all_to_all | solution.py:72
  102.2 0.5 convolution_bitcast_fusion.1
  102.7 0.6 fusion.4
  103.3 1.8 %fusion.42 = f32[128,256]{1,0:T(8,128)S(1)} fusion(f32[1,128,256]{1,2,0:T(8,128)S(1)} %fusion.4, f32[1,128,256]{1,2,0:T(8,128)S(1)} %convolution_bitcast_fusion.1), kind=kOutput, calls=%fused_computation.65 | convolution fusion | flops 102137856 | bytes 393216 | tf_op jit(solution)/shard_map/cas,sb->cab/dot_general | solution.py:32
  105.1 1.8 %fusion.38 = f32[128,256]{1,0:T(8,128)S(1)} fusion(f32[1,128,256]{1,2,0:T(8,128)S(1)} %convolution_bitcast_fusion.1, f32[1,128,256]{1,2,0:T(8,128)S(1)} %fusion.4), kind=kOutput, calls=%fused_computation.61 | convolution fusion | flops 102137856 | bytes 393216 | tf_op jit(solution)/shard_map/cas,sb->cab/dot_general | solution.py:35
  106.9 1.8 %convolution_add_fusion.2 = f32[128,256]{1,0:T(8,128)S(1)} fusion(f32[128,256]{1,0:T(8,128)S(1)} %fusion.42, f32[1,128,256]{1,2,0:T(8,128)S(1)} %convolution_bitcast_fusion.1, f32[1,128,256]{1,2,0:T(8,128)S(1)} %fusion.4), kind=kOutput, calls=%fused_computation.9 | convolution fusion | flops 102170624 | bytes 524288 | tf_op jit(solution)/shard_map/cas,sb->cab/dot_general | solution.py:32
  108.7 1.8 %multiply_add_fusion = (f32[128,256]{1,0:T(8,128)S(1)}, f32[128,256]{1,0:T(8,128)S(1)}) fusion(f32[128,256]{1,0:T(8,128)S(1)} %convolution_add_fusion.1, f32[128,256]{1,0:T(8,128)S(1)} %convolution_add_fusion.2, f32[128,256]{1,0:T(8,128)S(1)} %convolution_subtract_fusion.1, f32[128,256]{1,0:T(8,128)S(1)} %fusion.38, f32[1,128,256]{1,2,0:T(8,128)S(1)} %fusion.4, ...), kind=kOutput, calls=%fused_computation.76 | convolution fusion | flops 102367232 | bytes 1048576 | tf_op jit(solution)/shard_map/cas,sb->cab/dot_general | solution.py:35
  110.6 1.2 fusion.56
  111.9 1.5 %fusion.62 = f32[128,256]{1,0:T(8,128)S(1)} fusion(f32[128,256]{1,0:T(8,128)S(1)} %get-tuple-element.6), kind=kOutput, calls=%fused_computation.84 | convolution fusion | flops 101580800 | bytes 262144 | tf_op jit(solution)/shard_map/cab,bs->cas/dot_general | solution.py:46
  113.3 1.3 convolution_subtract_fusion
  114.6 1.2 convolution_add_fusion
  115.9 1.1 fusion.47
  117.0 0.1 copy.11
  117.1 1.1 fusion.7
  118.2 0.1 copy.14
  118.3 14.1 %all_to_all.29 = f32[1,128,256]{2,0,1:T(1,128)S(1)} all-to-all(f32[1,128,256]{2,0,1:T(1,128)S(1)} %copy.14), channel_id=1, replica_groups=mesh['tm'=8,'nrn'=16] {'tm','nrn'}, dimensions={1} | all-to-all | bytes 262144 | tf_op jit(solution)/shard_map/all_to_all | solution.py:83
  132.3 0.1 copy.15
  132.4 0.1 fusion.29
  132.6 0.0 copy-done.2
  132.6 0.0 copy-done.3
  132.6 0.3 fusion.77
  132.9 0.0 copy-done.4
  132.9 0.0 copy-done.5
  132.9 1.1 fusion.8
  (2 shorter events, 0.0 us)
Async XLA Ops:
  6.5 1.0 copy-start
  6.5 11.0 %copy-start.1 = (f32[1,32768]{1,0:T(1,128)S(1)}, f32[1,32768]{1,0:T(1,128)}, u32[]{:S(2)}) copy-start(f32[1,32768]{1,0:T(1,128)} %param.9) | copy-start | bytes 393220
  6.5 73.6 %reduce-scatter.2.cloned.1.call-start = ((), (), s32[]{:S(2)}) async-start(), calls=%async_computation.3 | async-start | bytes 2228224 | tf_op jit(solution)/shard_map/reduce_scatter | solution.py:65
  17.0 115.6 %copy-start.2 = (bf16[128,512]{1,0:T(8,128)(2,1)S(1)}, bf16[128,512]{1,0:T(8,128)(2,1)}, u32[]{:S(2)}) copy-start(bf16[128,512]{1,0:T(8,128)(2,1)} %param.11) | copy-start | bytes 393220
  17.0 115.6 %copy-start.3 = (f32[128]{0:T(128)S(1)}, f32[128]{0:T(128)}, u32[]{:S(2)}) copy-start(f32[128]{0:T(128)} %param.10) | copy-start | bytes 1540
  17.0 115.8 %copy-start.4 = (bf16[512,128]{1,0:T(8,128)(2,1)S(1)}, bf16[512,128]{1,0:T(8,128)(2,1)}, u32[]{:S(2)}) copy-start(bf16[512,128]{1,0:T(8,128)(2,1)} %param.13) | copy-start | bytes 393220
  17.0 115.8 %copy-start.5 = (bf16[128,512]{1,0:T(8,128)(2,1)S(1)}, bf16[128,512]{1,0:T(8,128)(2,1)}, u32[]{:S(2)}) copy-start(bf16[128,512]{1,0:T(8,128)(2,1)} %param.12) | copy-start | bytes 393220
  81.8 20.4 %all-to-all-start = ((f32[128,1,256]{2,1,0:T(1,128)}), f32[128,1,256]{2,1,0:T(1,128)S(1)}, u32[]{:S(2)}, u32[]{:S(2)}) async-start(f32[128,1,256]{2,1,0:T(1,128)} %copy.10), calls=%async_computation.1 | async-start | bytes 262144 | tf_op jit(solution)/shard_map/all_to_all | solution.py:72
Sparse Core Ops, SparseCore 0:
  17.2 62.8 reduce-scatter.1
where the time goes:
time: 141 us
  waiting for transfers between devices  62.8 us (45%)
  matrix products  34.9 us (25%)
  blocking collectives  14.1 us (10%)
  between operations  13.6 us (10%)
  starting transfers between devices  10.8 us (8%)
  local copies, waits for them, and re-layouts  3.56 us (3%)
    reduce_scatter x1, waiting for transfers between devices, per_device(): lax.psum_scatter(jnp.dot(spikes, read_in, preferred_element_type=jnp.floa...  55 us
    all_to_all x1, blocking collectives, per_device(): lax.all_to_all(mixed, ('tm', 'nrn'), split_axis=1, concat_axis=0, tiled=T...  14.1 us
    all_to_all x1, starting transfers between devices, per_device(): lax.all_to_all(flipped, ('tm', 'nrn'), split_axis=0, concat_axis=1, tiled...  10.8 us
    dot_general x1, matrix products, per_device(): jnp.dot(spikes, read_in, preferred_element_type=jnp.float32)  9.45 us
    all_to_all x1, waiting for transfers between devices, per_device(): lax.all_to_all(flipped, ('tm', 'nrn'), split_axis=0, concat_axis=1, tiled...  7.81 us
    dot_general x2, matrix products, forward_dft(): jnp.einsum('cas,sb->cab', twist_real, sin_inner, precision=precise)  3.66 us
    dot_general x2, matrix products, forward_dft(): jnp.einsum('cas,sb->cab', twist_imag, sin_inner, precision=precise)  3.64 us
    dot_general x2, matrix products, forward_dft(): jnp.einsum('cas,sb->cab', twist_real, cos_inner, precision=precise)  3.62 us
  transfers between devices with their start and end apart: 2, of which 2 were waited for; matrix products, arithmetic and copies ran while one was open for 7% of the time, Pallas kernels for 0%

commit v1 on v0

v1 whole, which is shorter than its diff:
```python
import math

import jax
import jax.numpy as jnp
import numpy as np
from jax import lax
from jax.experimental import pallas as pl
from jax.experimental.pallas import tpu as pltpu
from jax.sharding import PartitionSpec as P

f32 = jnp.float32
bf16 = jnp.bfloat16
LANES = 128


def split(table):
    table = np.asarray(table, np.float32)
    high = table.astype(jnp.bfloat16)
    low = (table - high.astype(np.float32)).astype(jnp.bfloat16)
    return jnp.asarray(high), jnp.asarray(low)


def dft_tables(rows):
    half = rows // 2 + 1
    padded = -(-half // 8) * 8
    total = rows * LANES
    a = np.arange(padded)
    keep = (a < half).astype(np.float64)
    row = np.arange(rows)
    angle = 2 * math.pi * ((a[:, None] * row[None, :]) % rows) / rows
    first = np.concatenate([np.cos(angle), -np.sin(angle)]) * np.tile(keep, 2)[:, None]
    lane = np.arange(LANES)
    angle = 2 * math.pi * ((a[:, None] * lane[None, :]) % total) / total
    twist_cos, twist_sin = np.cos(angle), np.sin(angle)
    angle = 2 * math.pi * ((lane[:, None] * lane[None, :]) % LANES) / LANES
    cos, sin = np.cos(angle), np.sin(angle)
    second = np.block([[cos, -sin], [sin, cos]])
    third = np.block([[cos, sin], [-sin, cos]])
    weight = np.where((a == 0) | (a == rows // 2), 1.0, 2.0) * keep
    angle = 2 * math.pi * ((row[:, None] * a[None, :]) % rows) / rows
    fourth = np.concatenate([np.cos(angle) * weight, -np.sin(angle) * weight], axis=1)
    return padded, first, twist_cos, twist_sin, second, third, fourth


def triple(left, right):
    (lh, ll), (rh, rl) = left, right
    dot = lambda p, q: jnp.dot(p, q, preferred_element_type=f32)
    return dot(lh, rh) + (dot(lh, rl) + dot(ll, rh))


def halves(value):
    high = value.astype(bf16)
    return high, (value - high.astype(f32)).astype(bf16)


def forward(signal, refs, padded):
    first_h, first_l, tc, ts, second_h, second_l = refs
    outer = triple((first_h[...], first_l[...]), halves(signal))
    real, imag = outer[:padded], outer[padded:]
    cos, sin = tc[...], ts[...]
    turned = jnp.concatenate([real * cos + imag * sin, imag * cos - real * sin], axis=1)
    return triple(halves(turned), (second_h[...], second_l[...]))


def project_kernel(core_ref, spikes_ref, read_ref, own_ref, other_ref, weight_ref):
    step = pl.program_id(0)
    width = read_ref.shape[1]

    @pl.when(step == 0)
    def _():
        channel = lax.broadcasted_iota(jnp.int32, (width, width), 0)
        place = lax.broadcasted_iota(jnp.int32, (width, width), 1)
        half = width // 2
        late = (place >= half).astype(jnp.int32)
        core = core_ref[0]
        wanted = 2 * (place - half * late) + (core + late - 2 * core * late)
        pick = jnp.where(channel == wanted, 1.0, 0.0).astype(bf16)
        weight_ref[...] = jnp.dot(read_ref[...], pick, preferred_element_type=f32).astype(bf16)

    part = jnp.dot(spikes_ref[...], weight_ref[...], preferred_element_type=f32)
    rows = part.shape[0] // LANES
    half = width // 2
    for k in range(rows):
        block = part[k * LANES : (k + 1) * LANES].T
        own_ref[:, step * rows + k, :] = block[:half]
        other_ref[:, step * rows + k, :] = block[half:]


def project(core, spikes, read_in, block):
    bins, neurons = spikes.shape
    width = read_in.shape[1]
    out = jax.ShapeDtypeStruct((width // 2, bins // LANES, LANES), f32)
    full = pl.BlockSpec(out.shape, lambda i, c: (0, 0, 0))
    return pl.pallas_call(
        project_kernel,
        out_shape=(out, out),
        grid_spec=pltpu.PrefetchScalarGridSpec(
            num_scalar_prefetch=1,
            grid=(bins // block,),
            in_specs=[
                pl.BlockSpec((block, neurons), lambda i, c: (i, 0)),
                pl.BlockSpec((neurons, width), lambda i, c: (0, 0)),
            ],
            out_specs=(full, full),
            scratch_shapes=[pltpu.VMEM((neurons, width), bf16)],
        ),
        compiler_params=pltpu.CompilerParams(
            dimension_semantics=("arbitrary",), vmem_limit_bytes=40 << 20
        ),
        name="project",
    )(core, spikes, read_in)


def spectrum_kernel(kern_ref, fh, fl, tc, ts, sh, sl, out_ref, *, padded, scale):
    out_ref[...] = forward(kern_ref[...], (fh, fl, tc, ts, sh, sl), padded) * scale


def convolve_kernel(
    parts_ref, spec_ref, fh, fl, tc, ts, sh, sl, th, tl, gh, gl, out_ref, *, padded, groups
):
    parts = parts_ref[...]
    each, lanes = parts.shape[1], parts.shape[2]
    members = parts.shape[0] // groups
    parts = parts.reshape(groups, members, each, lanes)
    series = parts[:, 0]
    for m in range(1, members):
        series = series + parts[:, m]
    series = series.reshape(groups * each, lanes)
    data = forward(series, (fh, fl, tc, ts, sh, sl), padded)
    dr, di = data[:, :LANES], data[:, LANES:]
    spec = spec_ref[...]
    kr, ki = spec[:, :LANES], spec[:, LANES:]
    prod = jnp.concatenate([dr * kr - di * ki, dr * ki + di * kr], axis=1)
    back = triple(halves(prod), (th[...], tl[...]))
    br, bi = back[:, :LANES], back[:, LANES:]
    cos, sin = tc[...], ts[...]
    turned = jnp.concatenate([br * cos - bi * sin, br * sin + bi * cos], axis=0)
    out_ref[...] = series + triple((gh[...], gl[...]), halves(turned))


def mlp_kernel(stack_ref, gain_ref, gate_ref, up_ref, down_ref, out_ref):
    channels = gate_ref.shape[0]
    each = stack_ref.shape[0] // channels
    residual = jnp.concatenate(
        [stack_ref[pl.ds(r, channels, stride=each), :].T for r in range(each)], axis=0
    )
    meansq = jnp.mean(residual * residual, axis=-1, keepdims=True)
    normed = (residual * lax.rsqrt(meansq + 1e-05) * gain_ref[...]).astype(bf16)
    gate = jnp.dot(normed, gate_ref[...], preferred_element_type=f32)
    upper = jnp.dot(normed, up_ref[...], preferred_element_type=f32)
    act = (gate / (1.0 + jnp.exp(-gate)) * upper).astype(bf16)
    out_ref[...] = (
        residual + jnp.dot(act, down_ref[...], preferred_element_type=f32)
    ).astype(bf16)


def per_device(spikes, read_in, kernel, gain, w_gate, w_up, w_down):
    time_groups = lax.axis_size("tm")
    neuron_groups = lax.axis_size("nrn")
    devices = time_groups * neuron_groups
    session = spikes.shape[0] * time_groups
    rows = session // LANES
    padded, first, twist_cos, twist_sin, second, third, fourth = dft_tables(rows)
    twist = (jnp.asarray(twist_cos, f32), jnp.asarray(twist_sin, f32))
    ahead = (*split(first), *twist, *split(second))
    core = (lax.axis_index("nrn") % 2).astype(jnp.int32).reshape(1)
    own, other = project(core, spikes, read_in, 512)
    swapped = lax.ppermute(other, "nrn", [(j, j ^ 1) for j in range(neuron_groups)])
    same = [[d for d in range(devices) if d % 2 == c] for c in range(2)]
    parts = lax.all_to_all(
        own + swapped, ("tm", "nrn"), 0, 0, tiled=True, axis_index_groups=same
    )
    spec = pl.pallas_call(
        lambda *refs: spectrum_kernel(*refs, padded=padded, scale=1.0 / session),
        out_shape=jax.ShapeDtypeStruct((padded, 2 * LANES), f32),
        name="spectrum",
    )(kernel.reshape(rows, LANES), *ahead)
    mixed = pl.pallas_call(
        lambda *refs: convolve_kernel(*refs, padded=padded, groups=time_groups),
        out_shape=jax.ShapeDtypeStruct((rows, LANES), f32),
        compiler_params=pltpu.CompilerParams(vmem_limit_bytes=40 << 20),
        name="convolve",
    )(parts, spec, *ahead, *split(third), *split(fourth))
    stacked = lax.all_to_all(
        mixed.reshape(devices, rows // devices, LANES), ("tm", "nrn"), 0, 0, tiled=True
    )
    return pl.pallas_call(
        mlp_kernel,
        out_shape=jax.ShapeDtypeStruct((rows * LANES // devices, gain.shape[0]), bf16),
        name="mlp",
    )(stacked.reshape(rows, LANES), gain.reshape(1, -1), w_gate, w_up, w_down)


def solution(mesh):
    placed = (P("tm", "nrn"), P("nrn", None), P(("tm", "nrn"), None), P(), P(), P(), P())
    return jax.shard_map(
        per_device, mesh=mesh, in_specs=placed, out_specs=P(("tm", "nrn"), None), check_vma=False
    )
```

time: 141 us -> 67.2 us (0.48)
  waiting for transfers between devices: 62.8 us -> 17.4 us
  matrix products: 34.9 us -> 0 us
  Pallas kernels: 0 us -> 17.6 us
  between operations: 13.6 us -> 0.14 us
  starting transfers between devices: 10.8 us -> 12.7 us
  blocking collectives: 14.1 us -> 15.8 us
  local copies, waits for them, and re-layouts: 3.56 us -> 2.03 us
    reduce_scatter x1 -> x0, waiting for transfers between devices: 55 us -> none  [per_device(): lax.psum_scatter(jnp.dot(spikes, read_in, preferred_element_type=jnp.floa...]
    dot_general x21 -> x0, matrix products: 34.9 us -> none  [the longest x1 9.45 us: per_device(): jnp.dot(spikes, read_in, preferred_element_type=jnp.float32)]
    pallas_call x0 -> x4, Pallas kernels: none -> 17.6 us  [the longest x1 11.6 us: project(): pl.pallas_call(project_kernel, out_shape=(out, out), grid_spec=pltpu.Pref...]
    all_to_all x1, waiting for transfers between devices: 7.81 us -> 15.1 us  [per_device(): lax.all_to_all(own + swapped, ('tm', 'nrn'), 0, 0, tiled=True, axis_index...]
    ppermute x0 -> x1, waiting for transfers between devices: none -> 2.29 us  [per_device(): lax.ppermute(other, 'nrn', [(j, j ^ 1) for j in range(neuron_groups)])]
    all_to_all x3 -> x0, local copies, waits for them, and re-layouts: 1.84 us -> none  [the longest x2 1.74 us: per_device(): lax.all_to_all(flipped, ('tm', 'nrn'), split_axis=0, concat_axis=1, tiled...]
    all_to_all x1, blocking collectives: 14.1 us -> 15.8 us  [per_device(): lax.all_to_all(mixed.reshape(devices, rows // devices, LANES), ('tm', 'nr...]
    ppermute x0 -> x1, starting transfers between devices: none -> 1.49 us  [per_device(): lax.ppermute(other, 'nrn', [(j, j ^ 1) for j in range(neuron_groups)])]
  transfers between devices with their start and end apart: 2 -> 2, of which waited for: 2 -> 2; matrix products, arithmetic and copies ran while one was open for 7% -> 0% of each run, Pallas kernels for 0% -> 4%
where the time goes in v1:
time: 67.2 us; the launch traced here: 66.8 us
  Pallas kernels  17.6 us (26%)
  waiting for transfers between devices  17.4 us (26%)
  blocking collectives  15.8 us (24%)
  starting transfers between devices  12.7 us (19%)
  local copies, waits for them, and re-layouts  2.03 us (3%)
  other arithmetic  1.19 us (2%)
    all_to_all x1, blocking collectives, per_device(): lax.all_to_all(mixed.reshape(devices, rows // devices, LANES), ('tm', 'nr...  15.8 us
    all_to_all x1, waiting for transfers between devices, per_device(): lax.all_to_all(own + swapped, ('tm', 'nrn'), 0, 0, tiled=True, axis_index...  15.1 us
    pallas_call x1, Pallas kernels, project(): pl.pallas_call(project_kernel, out_shape=(out, out), grid_spec=pltpu.Pref...  11.6 us
    all_to_all x1, starting transfers between devices, per_device(): lax.all_to_all(own + swapped, ('tm', 'nrn'), 0, 0, tiled=True, axis_index...  11.2 us
    pallas_call x1, Pallas kernels, per_device(): pl.pallas_call(mlp_kernel, out_shape=jax.ShapeDtypeStruct((rows * LANES /...  2.44 us
    pallas_call x1, Pallas kernels, per_device(): pl.pallas_call(lambda *refs: spectrum_kernel(*refs, padded=padded, scale=...  2.42 us
    ppermute x1, waiting for transfers between devices, per_device(): lax.ppermute(other, 'nrn', [(j, j ^ 1) for j in range(neuron_groups)])  2.29 us
    unnamed x24, local copies, waits for them, and re-layouts  2.03 us
  transfers between devices with their start and end apart: 2, of which 2 were waited for; matrix products, arithmetic and copies ran while one was open for 0% of the time, Pallas kernels for 4%

profile of v1, /device:TPU:1, one launch (start us, length us, event | category | flops | bytes accessed | tf_op | source)
XLA Modules:
  0.0 66.8 jit_solution(18239043719592113109)
XLA Ops:
  0.0 0.0 copy-start
  0.0 0.0 copy-start.1
  0.0 0.0 copy-start.3
  0.0 1.1 %copy-done.3 = bf16[2048,128]{1,0:T(8,128)(2,1)S(1)} copy-done((bf16[2048,128]{1,0:T(8,128)(2,1)S(1)}, bf16[2048,128]{1,0:T(8,128)(2,1)}, u32[]{:S(2)}) %copy-start.3) | copy-done | bytes 524312
  1.1 0.0 copy-start.4
  1.1 0.0 copy-start.5
  1.1 0.0 copy-start.6
  1.1 0.0 copy-start.7
  1.1 0.0 copy-start.8
  1.1 0.0 copy-start.9
  1.1 0.0 copy-start.10
  1.1 0.0 copy-start.11
  1.2 11.6 %project.1 = (f32[64,32,128]{2,1,0:T(8,128)S(1)}, f32[64,32,128]{2,1,0:T(8,128)S(1)}) custom-call(s32[1]{0:T(128)} %bitcast.core_ref, bf16[4096,2048]{1,0:T(8,128)(2,1)} %spikes_ref.1, bf16[2048,128]{1,0:T(8,128)(2,1)S(1)} %copy-done.3), custom_call_target="tpu_custom_call" | custom-call | tf_op jit(solution)/shard_map/project/pallas_call | solution.py:94
  12.8 1.5 %collective-permute-start = (f32[64,32,128]{2,1,0:T(8,128)S(1)}, f32[64,32,128]{2,1,0:T(8,128)S(1)}, u32[]{:S(2)}, u32[]{:S(2)}) collective-permute-start(f32[64,32,128]{2,1,0:T(8,128)S(1)} %get-tuple-element.8), channel_id=1, source_target_pairs={{0,1},{1,0},{2,3},{3,2},{4,5},{5,4},{6,7},{7,6},{8,9},{9,8},{10,11... | collective-permute-start | bytes 3145736 | tf_op jit(solution)/shard_map/ppermute | solution.py:168
  14.3 2.3 %collective-permute-done = f32[64,32,128]{2,1,0:T(8,128)S(1)} collective-permute-done((f32[64,32,128]{2,1,0:T(8,128)S(1)}, f32[64,32,128]{2,1,0:T(8,128)S(1)}, u32[]{:S(2)}, u32[]{:S(2)}) %collective-permute-start) | collective-permute-done | bytes 1048608 | tf_op jit(solution)/shard_map/ppermute | solution.py:168
  16.6 1.2 %add.8 = f32[64,32,128]{2,1,0:T(8,128)} add(f32[64,32,128]{2,1,0:T(8,128)S(1)} %get-tuple-element.7, f32[64,32,128]{2,1,0:T(8,128)S(1)} %collective-permute-done) | non-fusion elementwise | flops 262144 | bytes 3145728 | tf_op jit(solution)/shard_map/add | solution.py:171
  17.7 11.2 %all-to-all-start = ((f32[64,32,128]{2,1,0:T(8,128)}), f32[64,32,128]{2,1,0:T(8,128)S(1)}, u32[]{:S(2)}, u32[]{:S(2)}) async-start(f32[64,32,128]{2,1,0:T(8,128)} %add.8), calls=%async_computation | async-start | bytes 2097152 | tf_op jit(solution)/shard_map/all_to_all | solution.py:170
  29.0 2.4 %spectrum.1.refs_1_ = f32[136,256]{1,0:T(8,128)} custom-call(f32[256,128]{1,0:T(8,128)} %bitcast.7, bf16[272,256]{1,0:T(8,128)(2,1)} %constant.39.clone.refs_1_.refs_2_, bf16[272,256]{1,0:T(8,128)(2,1)} %constant.40.clone.refs_2_.refs_3_, f32[136,128]{1,0:T(8,128)} %constant.37.clone.refs_3_.refs_4_, f32[136,128]{1,0:T(8,128)} %constant.38.clone.refs_4_.refs_5_, ...), custom_call_target="tpu_custom_call" | custom-call | tf_op jit(solution)/shard_map/spectrum/pallas_call | solution.py:173
  31.4 15.1 %all-to-all-done.refs_0_ = f32[64,32,128]{2,1,0:T(8,128)S(1)} async-done(((f32[64,32,128]{2,1,0:T(8,128)}), f32[64,32,128]{2,1,0:T(8,128)S(1)}, u32[]{:S(2)}, u32[]{:S(2)}) %all-to-all-start) | async-done | bytes 1048608 | tf_op jit(solution)/shard_map/all_to_all | solution.py:170
  46.5 0.0 copy-done
  46.5 0.0 copy-done.1
  46.5 0.0 copy-done.4
  46.5 0.0 copy-done.5
  46.5 0.0 copy-done.6
  46.5 0.0 copy-done.7
  46.5 0.0 copy-done.8
  46.5 0.0 copy-done.9
  46.5 0.0 copy-done.10
  46.5 0.0 copy-done.11
  46.6 0.0 copy-start.2
  46.6 0.9 %copy-done.2 = f32[136,256]{1,0:T(8,128)S(1)} copy-done((f32[136,256]{1,0:T(8,128)S(1)}, f32[136,256]{1,0:T(8,128)}, u32[]{:S(2)}) %copy-start.2) | copy-done | bytes 139288
  47.5 1.1 %convolve.1 = f32[256,128]{1,0:T(8,128)S(1)} custom-call(f32[64,32,128]{2,1,0:T(8,128)S(1)} %all-to-all-done.refs_0_, f32[136,256]{1,0:T(8,128)S(1)} %copy-done.2, bf16[272,256]{1,0:T(8,128)(2,1)S(1)} %copy-done, bf16[272,256]{1,0:T(8,128)(2,1)S(1)} %copy-done.1, f32[136,128]{1,0:T(8,128)S(1)} %copy-done.6, f32[136,128]{1,0:T(8,128)S(1)} %copy-done.7, ...), custom_call_target="tpu_custom_call" | custom-call | tf_op jit(solution)/shard_map/convolve/pallas_call | solution.py:178
  48.5 15.8 %all_to_all.10 = f32[128,2,128]{2,1,0:T(2,128)} all-to-all(f32[128,2,128]{2,1,0:T(2,128)S(1)} %bitcast.5), channel_id=1, replica_groups=mesh['tm'=8,'nrn'=16] {'tm','nrn'}, dimensions={0} | all-to-all | bytes 262144 | tf_op jit(solution)/shard_map/all_to_all | solution.py:184
  64.3 2.4 %mlp.1 = bf16[256,128]{1,0:T(8,128)(2,1)} custom-call(f32[256,128]{1,0:T(8,128)} %bitcast.6, f32[1,128]{1,0:T(1,128)} %bitcast.8, bf16[128,512]{1,0:T(8,128)(2,1)} %gate_ref.1, bf16[128,512]{1,0:T(8,128)(2,1)} %up_ref.1, bf16[512,128]{1,0:T(8,128)(2,1)} %down_ref.1), custom_call_target="tpu_custom_call" | custom-call | tf_op jit(solution)/shard_map/mlp/pallas_call | solution.py:187
Async XLA Ops:
  0.0 46.5 %copy-start = (bf16[272,256]{1,0:T(8,128)(2,1)S(1)}, bf16[272,256]{1,0:T(8,128)(2,1)}, u32[]{:S(2)}) copy-start(bf16[272,256]{1,0:T(8,128)(2,1)} %constant.39.clone.refs_1_.refs_2_) | copy-start | bytes 417796
  0.0 46.5 %copy-start.1 = (bf16[272,256]{1,0:T(8,128)(2,1)S(1)}, bf16[272,256]{1,0:T(8,128)(2,1)}, u32[]{:S(2)}) copy-start(bf16[272,256]{1,0:T(8,128)(2,1)} %constant.40.clone.refs_2_.refs_3_) | copy-start | bytes 417796
  0.0 1.1 %copy-start.3 = (bf16[2048,128]{1,0:T(8,128)(2,1)S(1)}, bf16[2048,128]{1,0:T(8,128)(2,1)}, u32[]{:S(2)}) copy-start(bf16[2048,128]{1,0:T(8,128)(2,1)} %read_ref.1) | copy-start | bytes 1572868
  1.1 45.4 %copy-start.4 = (bf16[256,256]{1,0:T(8,128)(2,1)S(1)}, bf16[256,256]{1,0:T(8,128)(2,1)}, u32[]{:S(2)}) copy-start(bf16[256,256]{1,0:T(8,128)(2,1)} %constant.41.clone.refs_5_.refs_6_) | copy-start | bytes 393220
  1.1 45.4 %copy-start.5 = (bf16[256,256]{1,0:T(8,128)(2,1)S(1)}, bf16[256,256]{1,0:T(8,128)(2,1)}, u32[]{:S(2)}) copy-start(bf16[256,256]{1,0:T(8,128)(2,1)} %constant.42.clone.refs_6_.refs_7_) | copy-start | bytes 393220
  1.1 45.4 %copy-start.6 = (f32[136,128]{1,0:T(8,128)S(1)}, f32[136,128]{1,0:T(8,128)}, u32[]{:S(2)}) copy-start(f32[136,128]{1,0:T(8,128)} %constant.37.clone.refs_3_.refs_4_) | copy-start | bytes 208900
  1.1 45.4 %copy-start.7 = (f32[136,128]{1,0:T(8,128)S(1)}, f32[136,128]{1,0:T(8,128)}, u32[]{:S(2)}) copy-start(f32[136,128]{1,0:T(8,128)} %constant.38.clone.refs_4_.refs_5_) | copy-start | bytes 208900
  1.1 45.4 %copy-start.8 = (bf16[256,272]{1,0:T(8,128)(2,1)S(1)}, bf16[256,272]{1,0:T(8,128)(2,1)}, u32[]{:S(2)}) copy-start(bf16[256,272]{1,0:T(8,128)(2,1)} %constant.45.clone.refs_10_) | copy-start | bytes 417796
  1.1 45.4 %copy-start.9 = (bf16[256,272]{1,0:T(8,128)(2,1)S(1)}, bf16[256,272]{1,0:T(8,128)(2,1)}, u32[]{:S(2)}) copy-start(bf16[256,272]{1,0:T(8,128)(2,1)} %constant.46.clone.refs_11_) | copy-start | bytes 417796
  1.1 45.4 %copy-start.10 = (bf16[256,256]{1,0:T(8,128)(2,1)S(1)}, bf16[256,256]{1,0:T(8,128)(2,1)}, u32[]{:S(2)}) copy-start(bf16[256,256]{1,0:T(8,128)(2,1)} %constant.43.clone.refs_8_) | copy-start | bytes 393220
  1.1 45.4 %copy-start.11 = (bf16[256,256]{1,0:T(8,128)(2,1)S(1)}, bf16[256,256]{1,0:T(8,128)(2,1)}, u32[]{:S(2)}) copy-start(bf16[256,256]{1,0:T(8,128)(2,1)} %constant.44.clone.refs_9_) | copy-start | bytes 393220
  12.8 3.8 %collective-permute-start = (f32[64,32,128]{2,1,0:T(8,128)S(1)}, f32[64,32,128]{2,1,0:T(8,128)S(1)}, u32[]{:S(2)}, u32[]{:S(2)}) collective-permute-start(f32[64,32,128]{2,1,0:T(8,128)S(1)} %get-tuple-element.8), channel_id=1, source_target_pairs={{0,1},{1,0},{2,3},{3,2},{4,5},{5,4},{6,7},{7,6},{8,9},{9,8},{10,11... | collective-permute-start | bytes 3145736 | tf_op jit(solution)/shard_map/ppermute | solution.py:168
  17.7 28.7 %all-to-all-start = ((f32[64,32,128]{2,1,0:T(8,128)}), f32[64,32,128]{2,1,0:T(8,128)S(1)}, u32[]{:S(2)}, u32[]{:S(2)}) async-start(f32[64,32,128]{2,1,0:T(8,128)} %add.8), calls=%async_computation | async-start | bytes 2097152 | tf_op jit(solution)/shard_map/all_to_all | solution.py:170
  46.6 0.9 %copy-start.2 = (f32[136,256]{1,0:T(8,128)S(1)}, f32[136,256]{1,0:T(8,128)}, u32[]{:S(2)}) copy-start(f32[136,256]{1,0:T(8,128)} %spectrum.1.refs_1_) | copy-start | bytes 417796

commit v2 on v1

--- a/solution.py
+++ b/solution.py
@@ -62,51 +62,71 @@
     return triple(halves(turned), (second_h[...], second_l[...]))
 
 
-def project_kernel(core_ref, spikes_ref, read_ref, own_ref, other_ref, weight_ref):
-    step = pl.program_id(0)
+def project_kernel(core_ref, spikes_hbm, read_hbm, own_ref, other_ref, *scratch, pieces):
+    spikes_ref, read_ref, weight_ref, arrived, read_arrived = scratch
     width = read_ref.shape[1]
-
-    @pl.when(step == 0)
-    def _():
-        channel = lax.broadcasted_iota(jnp.int32, (width, width), 0)
-        place = lax.broadcasted_iota(jnp.int32, (width, width), 1)
-        half = width // 2
-        late = (place >= half).astype(jnp.int32)
-        core = core_ref[0]
-        wanted = 2 * (place - half * late) + (core + late - 2 * core * late)
-        pick = jnp.where(channel == wanted, 1.0, 0.0).astype(bf16)
-        weight_ref[...] = jnp.dot(read_ref[...], pick, preferred_element_type=f32).astype(bf16)
-
-    part = jnp.dot(spikes_ref[...], weight_ref[...], preferred_element_type=f32)
-    rows = part.shape[0] // LANES
     half = width // 2
-    for k in range(rows):
-        block = part[k * LANES : (k + 1) * LANES].T
-        own_ref[:, step * rows + k, :] = block[:half]
-        other_ref[:, step * rows + k, :] = block[half:]
-
-
-def project(core, spikes, read_in, block):
+    starts = [sum(pieces[:i]) for i in range(len(pieces))]
+    fetch_read = pltpu.make_async_copy(read_hbm, read_ref, read_arrived)
+    fetch_read.start()
+    fetches = [
+        pltpu.make_async_copy(
+            spikes_hbm.at[pl.ds(first, size)], spikes_ref.at[pl.ds(first, size)], arrived.at[i]
+        )
+        for i, (first, size) in enumerate(zip(starts, pieces))
+    ]
+    for fetch in fetches[:2]:
+        fetch.start()
+    fetch_read.wait()
+    channel = lax.broadcasted_iota(jnp.int32, (width, width), 0)
+    place = lax.broadcasted_iota(jnp.int32, (width, width), 1)
+    late = (place >= half).astype(jnp.int32)
+    core = core_ref[0]
+    wanted = 2 * (place - half * late) + (core + late - 2 * core * late)
+    pick = jnp.where(channel == wanted, 1.0, 0.0).astype(bf16)
+    weight_ref[...] = jnp.dot(read_ref[...], pick, preferred_element_type=f32).astype(bf16)
+
+    def put(part, block):
+        turned = part.T
+        own_ref[:, block, :] = turned[:half]
+        other_ref[:, block, :] = turned[half:]
+
+    held = None
+    for i, (first, size) in enumerate(zip(starts, pieces)):
+        fetches[i].wait()
+        if i + 2 < len(pieces):
+            fetches[i + 2].start()
+        for row in range(first, first + size, LANES):
+            part = jnp.dot(
+                spikes_ref[pl.ds(row, LANES)], weight_ref[...], preferred_element_type=f32
+            )
+            if held is not None:
+                put(*held)
+            held = (part, row // LANES)
+    put(*held)
+
+
+def project(core, spikes, read_in):
     bins, neurons = spikes.shape
     width = read_in.shape[1]
     out = jax.ShapeDtypeStruct((width // 2, bins // LANES, LANES), f32)
-    full = pl.BlockSpec(out.shape, lambda i, c: (0, 0, 0))
+    pieces = [bins // 8] + [bins // 4] * 3 + [bins // 8]
     return pl.pallas_call(
-        project_kernel,
+        lambda *refs: project_kernel(*refs, pieces=pieces),
         out_shape=(out, out),
-        grid_spec=pltpu.PrefetchScalarGridSpec(
-            num_scalar_prefetch=1,
-            grid=(bins // block,),
-            in_specs=[
-                pl.BlockSpec((block, neurons), lambda i, c: (i, 0)),
-                pl.BlockSpec((neurons, width), lambda i, c: (0, 0)),
-            ],
-            out_specs=(full, full),
-            scratch_shapes=[pltpu.VMEM((neurons, width), bf16)],
-        ),
-        compiler_params=pltpu.CompilerParams(
-            dimension_semantics=("arbitrary",), vmem_limit_bytes=40 << 20
-        ),
+        in_specs=[
+            pl.BlockSpec(memory_space=pltpu.SMEM),
+            pl.BlockSpec(memory_space=pltpu.HBM),
+            pl.BlockSpec(memory_space=pltpu.HBM),
+        ],
+        scratch_shapes=[
+            pltpu.VMEM((bins, neurons), bf16),
+            pltpu.VMEM((neurons, width), bf16),
+            pltpu.VMEM((neurons, width), bf16),
+            pltpu.SemaphoreType.DMA((len(pieces),)),
+            pltpu.SemaphoreType.DMA,
+        ],
+        compiler_params=pltpu.CompilerParams(vmem_limit_bytes=24 << 20),
         name="project",
     )(core, spikes, read_in)
 
@@ -164,21 +184,26 @@
     twist = (jnp.asarray(twist_cos, f32), jnp.asarray(twist_sin, f32))
     ahead = (*split(first), *twist, *split(second))
     core = (lax.axis_index("nrn") % 2).astype(jnp.int32).reshape(1)
-    own, other = project(core, spikes, read_in, 512)
+    spikes, read_in = (
+        pltpu.with_memory_space_constraint(x, pltpu.HBM) for x in (spikes, read_in)
+    )
+    own, other = project(core, spikes, read_in)
     swapped = lax.ppermute(other, "nrn", [(j, j ^ 1) for j in range(neuron_groups)])
+    spec = pl.pallas_call(
+        lambda *refs: spectrum_kernel(*refs, padded=padded, scale=1.0 / session),
+        out_shape=jax.ShapeDtypeStruct((padded, 2 * LANES), f32),
+        compiler_params=pltpu.CompilerParams(vmem_limit_bytes=8 << 20),
+        name="spectrum",
+    )(kernel.reshape(rows, LANES), *ahead)
+    swapped, spec = lax.optimization_barrier((swapped, spec))
     same = [[d for d in range(devices) if d % 2 == c] for c in range(2)]
     parts = lax.all_to_all(
         own + swapped, ("tm", "nrn"), 0, 0, tiled=True, axis_index_groups=same
     )
-    spec = pl.pallas_call(
-        lambda *refs: spectrum_kernel(*refs, padded=padded, scale=1.0 / session),
-        out_shape=jax.ShapeDtypeStruct((padded, 2 * LANES), f32),
-        name="spectrum",
-    )(kernel.reshape(rows, LANES), *ahead)
     mixed = pl.pallas_call(
         lambda *refs: convolve_kernel(*refs, padded=padded, groups=time_groups),
         out_shape=jax.ShapeDtypeStruct((rows, LANES), f32),
-        compiler_params=pltpu.CompilerParams(vmem_limit_bytes=40 << 20),
+        compiler_params=pltpu.CompilerParams(vmem_limit_bytes=12 << 20),
         name="convolve",
     )(parts, spec, *ahead, *split(third), *split(fourth))
     stacked = lax.all_to_all(
@@ -187,6 +212,7 @@
     return pl.pallas_call(
         mlp_kernel,
         out_shape=jax.ShapeDtypeStruct((rows * LANES // devices, gain.shape[0]), bf16),
+        compiler_params=pltpu.CompilerParams(vmem_limit_bytes=12 << 20),
         name="mlp",
     )(stacked.reshape(rows, LANES), gain.reshape(1, -1), w_gate, w_up, w_down)
 

time: 67.2 us -> 59.1 us (0.88)
  blocking collectives: 15.8 us -> 43.7 us
  waiting for transfers between devices: 17.4 us -> 1.7 us
  starting transfers between devices: 12.7 us -> 1.5 us
  Pallas kernels: 17.6 us -> 11.6 us
  local copies, waits for them, and re-layouts: 2.03 us -> 0.08 us
  other arithmetic: 1.19 us -> 0.21 us
    all_to_all x0 -> x1, blocking collectives: none -> 28.5 us  [per_device(): lax.all_to_all(own + swapped, ('tm', 'nrn'), 0, 0, tiled=True, axis_index...]
    all_to_all x1 -> x0, waiting for transfers between devices: 15.1 us -> none  [per_device(): lax.all_to_all(own + swapped, ('tm', 'nrn'), 0, 0, tiled=True, axis_index...]
    all_to_all x1 -> x0, starting transfers between devices: 11.2 us -> none  [per_device(): lax.all_to_all(own + swapped, ('tm', 'nrn'), 0, 0, tiled=True, axis_index...]
    pallas_call x1, Pallas kernels: 11.6 us -> 8.62 us  [project(): pl.pallas_call(lambda *refs: project_kernel(*refs, pieces=pieces), out_sh...]
    unnamed x24 -> x30, local copies, waits for them, and re-layouts: 2.03 us -> 0.08 us
    pallas_call x1, Pallas kernels: 2.42 us -> 0.54 us  [per_device(): pl.pallas_call(lambda *refs: spectrum_kernel(*refs, padded=padded, scale=...]
    pallas_call x1, Pallas kernels: 2.44 us -> 1.32 us  [per_device(): pl.pallas_call(mlp_kernel, out_shape=jax.ShapeDtypeStruct((rows * LANES /...]
    add x1, other arithmetic: 1.19 us -> 0.21 us  [per_device(): own + swapped]
  transfers between devices with their start and end apart: 2 -> 1, of which waited for: 2 -> 1; matrix products, arithmetic and copies ran while one was open for 0% -> 0% of each run, Pallas kernels for 4% -> 1%
where the time goes in v2:
time: 59.1 us; the launch traced here: 59 us
  blocking collectives  43.7 us (74%)
  Pallas kernels  11.6 us (20%)
  waiting for transfers between devices  1.7 us (3%)
  starting transfers between devices  1.5 us (3%)
    all_to_all x1, blocking collectives, per_device(): lax.all_to_all(own + swapped, ('tm', 'nrn'), 0, 0, tiled=True, axis_index...  28.5 us
    all_to_all x1, blocking collectives, per_device(): lax.all_to_all(mixed.reshape(devices, rows // devices, LANES), ('tm', 'nr...  15.2 us
    pallas_call x1, Pallas kernels, project(): pl.pallas_call(lambda *refs: project_kernel(*refs, pieces=pieces), out_sh...  8.62 us
    ppermute x1, waiting for transfers between devices, per_device(): lax.ppermute(other, 'nrn', [(j, j ^ 1) for j in range(neuron_groups)])  1.7 us
    ppermute x1, starting transfers between devices, per_device(): lax.ppermute(other, 'nrn', [(j, j ^ 1) for j in range(neuron_groups)])  1.5 us
    pallas_call x1, Pallas kernels, per_device(): pl.pallas_call(mlp_kernel, out_shape=jax.ShapeDtypeStruct((rows * LANES /...  1.32 us
  transfers between devices with their start and end apart: 1, of which 1 were waited for; matrix products, arithmetic and copies ran while one was open for 0% of the time, Pallas kernels for 1%

profile of v2, /device:TPU:1, one launch (start us, length us, event | category | flops | bytes accessed | tf_op | source)
XLA Modules:
  0.0 59.0 jit_solution(1344959391215973784)
XLA Ops:
  0.0 0.0 copy-start.4
  0.0 0.0 copy-start.5
  0.0 0.0 copy-start
  0.0 0.0 copy-start.1
  0.0 0.0 copy-start.2
  0.0 0.0 copy-start.3
  0.0 0.0 copy-start.12
  0.1 0.0 copy-start.13
  0.1 0.0 copy-start.6
  0.1 0.0 copy-start.7
  0.1 0.0 copy-start.11
  0.1 0.0 copy-start.14
  0.1 0.0 copy-start.8
  0.1 0.0 copy-start.9
  0.1 0.0 copy-start.10
  0.2 8.6 %project.1 = (f32[64,32,128]{2,1,0:T(8,128)S(1)}, f32[64,32,128]{2,1,0:T(8,128)S(1)}) custom-call(s32[1]{0:T(128)} %bitcast.refs_0_, bf16[4096,2048]{1,0:T(8,128)(2,1)} %refs_1_.2, bf16[2048,128]{1,0:T(8,128)(2,1)} %refs_2_.3), custom_call_target="tpu_custom_call" | custom-call | tf_op jit(solution)/shard_map/project/pallas_call | solution.py:114
  8.8 1.5 %collective-permute-start = (f32[64,32,128]{2,1,0:T(8,128)S(1)}, f32[64,32,128]{2,1,0:T(8,128)S(1)}, u32[]{:S(2)}, u32[]{:S(2)}) collective-permute-start(f32[64,32,128]{2,1,0:T(8,128)S(1)} %get-tuple-element.10), channel_id=1, source_target_pairs={{0,1},{1,0},{2,3},{3,2},{4,5},{5,4},{6,7},{7,6},{8,9},{9,8},{10,11... | collective-permute-start | bytes 3145736 | tf_op jit(solution)/shard_map/ppermute | solution.py:191
  10.3 0.0 copy-done.4
  10.3 0.0 copy-done.5
  10.3 0.0 copy-done
  10.3 0.0 copy-done.1
  10.3 0.0 copy-done.2
  10.3 0.0 copy-done.3
  10.3 0.0 copy-done.11
  10.3 0.5 spectrum.1.refs_1_
  10.9 1.7 %collective-permute-done = f32[64,32,128]{2,1,0:T(8,128)S(1)} collective-permute-done((f32[64,32,128]{2,1,0:T(8,128)S(1)}, f32[64,32,128]{2,1,0:T(8,128)S(1)}, u32[]{:S(2)}, u32[]{:S(2)}) %collective-permute-start) | collective-permute-done | bytes 1048608 | tf_op jit(solution)/shard_map/ppermute | solution.py:191
  12.6 0.2 add.8
  12.8 28.5 %all_to_all.10.refs_0_ = f32[64,32,128]{2,1,0:T(8,128)S(1)} all-to-all(f32[64,32,128]{2,1,0:T(8,128)S(1)} %add.8), channel_id=1, replica_groups={{0,2,4,6,8,10,12,14,16,18,20,22,24,26,28,30,32,34,36,38,40,42,44,46,48,..., dimensions={0} | all-to-all | bytes 2097152 | tf_op jit(solution)/shard_map/all_to_all | solution.py:200
  41.3 0.0 copy-done.12
  41.3 0.0 copy-done.13
  41.3 0.0 copy-done.6
  41.3 0.0 copy-done.7
  41.3 1.1 %convolve.1 = f32[256,128]{1,0:T(8,128)S(1)} custom-call(f32[64,32,128]{2,1,0:T(8,128)S(1)} %all_to_all.10.refs_0_, f32[136,256]{1,0:T(8,128)S(1)} %spectrum.1.refs_1_, bf16[272,256]{1,0:T(8,128)(2,1)S(1)} %copy-done, bf16[272,256]{1,0:T(8,128)(2,1)S(1)} %copy-done.1, f32[136,128]{1,0:T(8,128)S(1)} %copy-done.4, f32[136,128]{1,0:T(8,128)S(1)} %copy-done.5, ...), custom_call_target="tpu_custom_call" | custom-call | tf_op jit(solution)/shard_map/convolve/pallas_call | solution.py:203
  42.4 15.2 %all_to_all.11 = f32[128,2,128]{2,1,0:T(2,128)S(1)} all-to-all(f32[128,2,128]{2,1,0:T(2,128)S(1)} %bitcast.6), channel_id=1, replica_groups=mesh['tm'=8,'nrn'=16] {'tm','nrn'}, dimensions={0} | all-to-all | bytes 262144 | tf_op jit(solution)/shard_map/all_to_all | solution.py:209
  57.6 0.0 copy-done.14
  57.6 0.0 copy-done.8
  57.6 0.0 copy-done.9
  57.6 0.0 copy-done.10
  57.6 1.3 %mlp.1 = bf16[256,128]{1,0:T(8,128)(2,1)} custom-call(f32[256,128]{1,0:T(8,128)S(1)} %bitcast.5, f32[1,128]{1,0:T(1,128)S(1)} %bitcast.8, bf16[128,512]{1,0:T(8,128)(2,1)S(1)} %copy-done.8, bf16[128,512]{1,0:T(8,128)(2,1)S(1)} %copy-done.9, bf16[512,128]{1,0:T(8,128)(2,1)S(1)} %copy-done.10), custom_call_target="tpu_custom_call" | custom-call | tf_op jit(solution)/shard_map/mlp/pallas_call | solution.py:212
Async XLA Ops:
  0.0 10.3 %copy-start.4 = (f32[136,128]{1,0:T(8,128)S(1)}, f32[136,128]{1,0:T(8,128)}, u32[]{:S(2)}) copy-start(f32[136,128]{1,0:T(8,128)} %constant.37.clone.refs_3_.refs_4_) | copy-start | bytes 208900
  0.0 10.3 %copy-start.5 = (f32[136,128]{1,0:T(8,128)S(1)}, f32[136,128]{1,0:T(8,128)}, u32[]{:S(2)}) copy-start(f32[136,128]{1,0:T(8,128)} %constant.38.clone.refs_4_.refs_5_) | copy-start | bytes 208900
  0.0 10.3 %copy-start = (bf16[272,256]{1,0:T(8,128)(2,1)S(1)}, bf16[272,256]{1,0:T(8,128)(2,1)}, u32[]{:S(2)}) copy-start(bf16[272,256]{1,0:T(8,128)(2,1)} %constant.39.clone.refs_1_.refs_2_) | copy-start | bytes 417796
  0.0 10.3 %copy-start.1 = (bf16[272,256]{1,0:T(8,128)(2,1)S(1)}, bf16[272,256]{1,0:T(8,128)(2,1)}, u32[]{:S(2)}) copy-start(bf16[272,256]{1,0:T(8,128)(2,1)} %constant.40.clone.refs_2_.refs_3_) | copy-start | bytes 417796
  0.0 10.3 %copy-start.2 = (bf16[256,256]{1,0:T(8,128)(2,1)S(1)}, bf16[256,256]{1,0:T(8,128)(2,1)}, u32[]{:S(2)}) copy-start(bf16[256,256]{1,0:T(8,128)(2,1)} %constant.41.clone.refs_5_.refs_6_) | copy-start | bytes 393220
  0.0 10.3 %copy-start.3 = (bf16[256,256]{1,0:T(8,128)(2,1)S(1)}, bf16[256,256]{1,0:T(8,128)(2,1)}, u32[]{:S(2)}) copy-start(bf16[256,256]{1,0:T(8,128)(2,1)} %constant.42.clone.refs_6_.refs_7_) | copy-start | bytes 393220
  0.0 41.3 %copy-start.12 = (bf16[256,256]{1,0:T(8,128)(2,1)S(1)}, bf16[256,256]{1,0:T(8,128)(2,1)}, u32[]{:S(2)}) copy-start(bf16[256,256]{1,0:T(8,128)(2,1)} %constant.43.clone.refs_8_) | copy-start | bytes 393220
  0.1 41.3 %copy-start.13 = (bf16[256,256]{1,0:T(8,128)(2,1)S(1)}, bf16[256,256]{1,0:T(8,128)(2,1)}, u32[]{:S(2)}) copy-start(bf16[256,256]{1,0:T(8,128)(2,1)} %constant.44.clone.refs_9_) | copy-start | bytes 393220
  0.1 41.2 %copy-start.6 = (bf16[256,272]{1,0:T(8,128)(2,1)S(1)}, bf16[256,272]{1,0:T(8,128)(2,1)}, u32[]{:S(2)}) copy-start(bf16[256,272]{1,0:T(8,128)(2,1)} %constant.45.clone.refs_10_) | copy-start | bytes 417796
  0.1 41.2 %copy-start.7 = (bf16[256,272]{1,0:T(8,128)(2,1)S(1)}, bf16[256,272]{1,0:T(8,128)(2,1)}, u32[]{:S(2)}) copy-start(bf16[256,272]{1,0:T(8,128)(2,1)} %constant.46.clone.refs_11_) | copy-start | bytes 417796
  0.1 10.2 %copy-start.11 = (f32[1,32768]{1,0:T(1,128)S(1)}, f32[1,32768]{1,0:T(1,128)}, u32[]{:S(2)}) copy-start(f32[1,32768]{1,0:T(1,128)} %param.19) | copy-start | bytes 393220
  0.1 57.5 %copy-start.14 = (f32[128]{0:T(128)S(1)}, f32[128]{0:T(128)}, u32[]{:S(2)}) copy-start(f32[128]{0:T(128)} %param.20) | copy-start | bytes 1540
  0.1 57.5 %copy-start.8 = (bf16[128,512]{1,0:T(8,128)(2,1)S(1)}, bf16[128,512]{1,0:T(8,128)(2,1)}, u32[]{:S(2)}) copy-start(bf16[128,512]{1,0:T(8,128)(2,1)} %gate_ref.1) | copy-start | bytes 393220
  0.1 57.5 %copy-start.9 = (bf16[128,512]{1,0:T(8,128)(2,1)S(1)}, bf16[128,512]{1,0:T(8,128)(2,1)}, u32[]{:S(2)}) copy-start(bf16[128,512]{1,0:T(8,128)(2,1)} %up_ref.1) | copy-start | bytes 393220
  0.1 57.5 %copy-start.10 = (bf16[512,128]{1,0:T(8,128)(2,1)S(1)}, bf16[512,128]{1,0:T(8,128)(2,1)}, u32[]{:S(2)}) copy-start(bf16[512,128]{1,0:T(8,128)(2,1)} %down_ref.1) | copy-start | bytes 393220
  8.8 3.8 %collective-permute-start = (f32[64,32,128]{2,1,0:T(8,128)S(1)}, f32[64,32,128]{2,1,0:T(8,128)S(1)}, u32[]{:S(2)}, u32[]{:S(2)}) collective-permute-start(f32[64,32,128]{2,1,0:T(8,128)S(1)} %get-tuple-element.10), channel_id=1, source_target_pairs={{0,1},{1,0},{2,3},{3,2},{4,5},{5,4},{6,7},{7,6},{8,9},{9,8},{10,11... | collective-permute-start | bytes 3145736 | tf_op jit(solution)/shard_map/ppermute | solution.py:191

commit v3 on v2

--- a/solution.py
+++ b/solution.py
@@ -62,11 +62,27 @@
     return triple(halves(turned), (second_h[...], second_l[...]))
 
 
-def project_kernel(core_ref, spikes_hbm, read_hbm, own_ref, other_ref, *scratch, pieces):
-    spikes_ref, read_ref, weight_ref, arrived, read_arrived = scratch
+def put(part, own_ref, other_ref, block):
+    turned = part.T
+    half = turned.shape[0] // 2
+    own_ref[:, block, :] = turned[:half]
+    other_ref[:, block, :] = turned[half:]
+
+
+def products(spikes_ref, weight, rows, own_ref, other_ref, held):
+    for row in rows:
+        part = jnp.dot(spikes_ref[pl.ds(row, LANES)], weight[...], preferred_element_type=f32)
+        if held is not None:
+            put(held[0], own_ref, other_ref, held[1])
+        held = (part, row // LANES)
+    return held
+
+
+def project_kernel(core_ref, spikes_hbm, read_hbm, own_ref, other_ref, rest_ref, weight_ref, *scratch, pieces):
+    spikes_ref, read_ref, arrived, read_arrived = scratch
     width = read_ref.shape[1]
     half = width // 2
-    starts = [sum(pieces[:i]) for i in range(len(pieces))]
+    starts = [sum(pieces[:i]) for i in range(len(pieces) + 1)]
     fetch_read = pltpu.make_async_copy(read_hbm, read_ref, read_arrived)
     fetch_read.start()
     fetches = [
@@ -75,6 +91,11 @@
         )
         for i, (first, size) in enumerate(zip(starts, pieces))
     ]
+    fetches.append(
+        pltpu.make_async_copy(
+            spikes_hbm.at[pl.ds(starts[-1], rest_ref.shape[0])], rest_ref, arrived.at[len(pieces)]
+        )
+    )
     for fetch in fetches[:2]:
         fetch.start()
     fetch_read.wait()
@@ -82,53 +103,65 @@
     place = lax.broadcasted_iota(jnp.int32, (width, width), 1)
     late = (place >= half).astype(jnp.int32)
     core = core_ref[0]
-    wanted = 2 * (place - half * late) + (core + late - 2 * core * late)
+    wanted = 2 * (half - 1 - (place - half * late)) + (core + late - 2 * core * late)
     pick = jnp.where(channel == wanted, 1.0, 0.0).astype(bf16)
     weight_ref[...] = jnp.dot(read_ref[...], pick, preferred_element_type=f32).astype(bf16)
-
-    def put(part, block):
-        turned = part.T
-        own_ref[:, block, :] = turned[:half]
-        other_ref[:, block, :] = turned[half:]
-
     held = None
     for i, (first, size) in enumerate(zip(starts, pieces)):
         fetches[i].wait()
-        if i + 2 < len(pieces):
+        if i + 2 < len(fetches):
             fetches[i + 2].start()
-        for row in range(first, first + size, LANES):
-            part = jnp.dot(
-                spikes_ref[pl.ds(row, LANES)], weight_ref[...], preferred_element_type=f32
-            )
-            if held is not None:
-                put(*held)
-            held = (part, row // LANES)
-    put(*held)
-
-
-def project(core, spikes, read_in):
+        rows = range(first, first + size, LANES)
+        held = products(spikes_ref, weight_ref, rows, own_ref, other_ref, held)
+    put(held[0], own_ref, other_ref, held[1])
+    fetches[-1].wait()
+
+
+def rest_kernel(rest_ref, weight_ref, own_ref, other_ref):
+    rows = range(0, rest_ref.shape[0], LANES)
+    held = products(rest_ref, weight_ref, rows, own_ref, other_ref, None)
+    put(held[0], own_ref, other_ref, held[1])
+
+
+def project(core, spikes, read_in, swap):
     bins, neurons = spikes.shape
     width = read_in.shape[1]
-    out = jax.ShapeDtypeStruct((width // 2, bins // LANES, LANES), f32)
-    pieces = [bins // 8] + [bins // 4] * 3 + [bins // 8]
-    return pl.pallas_call(
+    part = lambda rows: jax.ShapeDtypeStruct((width // 2, rows // LANES, LANES), f32)
+    pieces = [bins // 8, bins // 4, bins // 4, bins // 8]
+    head = sum(pieces)
+    tail = bins - head
+    vmem = pl.BlockSpec(memory_space=pltpu.VMEM)
+    own, other, rest, weight = pl.pallas_call(
         lambda *refs: project_kernel(*refs, pieces=pieces),
-        out_shape=(out, out),
+        out_shape=(
+            part(head),
+            part(head),
+            jax.ShapeDtypeStruct((tail, neurons), bf16),
+            jax.ShapeDtypeStruct((neurons, width), bf16),
+        ),
         in_specs=[
             pl.BlockSpec(memory_space=pltpu.SMEM),
             pl.BlockSpec(memory_space=pltpu.HBM),
             pl.BlockSpec(memory_space=pltpu.HBM),
         ],
+        out_specs=(vmem,) * 4,
         scratch_shapes=[
-            pltpu.VMEM((bins, neurons), bf16),
+            pltpu.VMEM((head, neurons), bf16),
             pltpu.VMEM((neurons, width), bf16),
-            pltpu.VMEM((neurons, width), bf16),
-            pltpu.SemaphoreType.DMA((len(pieces),)),
+            pltpu.SemaphoreType.DMA((len(pieces) + 1,)),
             pltpu.SemaphoreType.DMA,
         ],
         compiler_params=pltpu.CompilerParams(vmem_limit_bytes=24 << 20),
         name="project",
     )(core, spikes, read_in)
+    swapped = swap(other)
+    own_rest, other_rest = pl.pallas_call(
+        rest_kernel,
+        out_shape=(part(tail), part(tail)),
+        compiler_params=pltpu.CompilerParams(vmem_limit_bytes=8 << 20),
+        name="rest",
+    )(rest, weight)
+    return own, swapped, own_rest, swap(other_rest)
 
 
 def spectrum_kernel(kern_ref, fh, fl, tc, ts, sh, sl, out_ref, *, padded, scale):
@@ -145,7 +178,7 @@
     series = parts[:, 0]
     for m in range(1, members):
         series = series + parts[:, m]
-    series = series.reshape(groups * each, lanes)
+    series = jnp.concatenate([series[g] for g in reversed(range(groups))], axis=0)
     data = forward(series, (fh, fl, tc, ts, sh, sl), padded)
     dr, di = data[:, :LANES], data[:, LANES:]
     spec = spec_ref[...]
@@ -187,19 +220,18 @@
     spikes, read_in = (
         pltpu.with_memory_space_constraint(x, pltpu.HBM) for x in (spikes, read_in)
     )
-    own, other = project(core, spikes, read_in)
-    swapped = lax.ppermute(other, "nrn", [(j, j ^ 1) for j in range(neuron_groups)])
+    swap = lambda x: lax.ppermute(x, "nrn", [(j, j ^ 1) for j in range(neuron_groups)])
+    own, swapped, own_rest, swapped_rest = project(core, spikes, read_in, swap)
     spec = pl.pallas_call(
         lambda *refs: spectrum_kernel(*refs, padded=padded, scale=1.0 / session),
         out_shape=jax.ShapeDtypeStruct((padded, 2 * LANES), f32),
         compiler_params=pltpu.CompilerParams(vmem_limit_bytes=8 << 20),
         name="spectrum",
     )(kernel.reshape(rows, LANES), *ahead)
-    swapped, spec = lax.optimization_barrier((swapped, spec))
-    same = [[d for d in range(devices) if d % 2 == c] for c in range(2)]
-    parts = lax.all_to_all(
-        own + swapped, ("tm", "nrn"), 0, 0, tiled=True, axis_index_groups=same
-    )
+    swapped_rest, spec = lax.optimization_barrier((swapped_rest, spec))
+    summed = jnp.concatenate([own + swapped, own_rest + swapped_rest], axis=1)
+    same = [[d for d in range(devices) if d % 2 == c][::-1] for c in range(2)]
+    parts = lax.all_to_all(summed, ("tm", "nrn"), 0, 0, tiled=True, axis_index_groups=same)
     mixed = pl.pallas_call(
         lambda *refs: convolve_kernel(*refs, padded=padded, groups=time_groups),
         out_shape=jax.ShapeDtypeStruct((rows, LANES), f32),

time: 59.1 us -> 58 us (0.981)
  waiting for transfers between devices: 1.7 us -> 0.91 us
  blocking collectives: 43.7 us -> 43.1 us
    all_to_all x1, blocking collectives: 28.5 us -> 24.9 us  [per_device(): lax.all_to_all(summed, ('tm', 'nrn'), 0, 0, tiled=True, axis_index_groups...]
    all_to_all x1, blocking collectives: 15.2 us -> 18.2 us  [per_device(): lax.all_to_all(mixed.reshape(devices, rows // devices, LANES), ('tm', 'nr...]
    pallas_call x0 -> x1, Pallas kernels: none -> 1.39 us  [project(): pl.pallas_call(rest_kernel, out_shape=(part(tail), part(tail)), compiler_...]
    pallas_call x1, Pallas kernels: 8.62 us -> 7.27 us  [project(): pl.pallas_call(lambda *refs: project_kernel(*refs, pieces=pieces), out_sh...]
    ppermute x1 -> x2, waiting for transfers between devices: 1.7 us -> 0.91 us  [per_device(): lax.ppermute(x, 'nrn', [(j, j ^ 1) for j in range(neuron_groups)])]
    ppermute x1 -> x2, starting transfers between devices: 1.5 us -> 1.59 us  [per_device(): lax.ppermute(x, 'nrn', [(j, j ^ 1) for j in range(neuron_groups)])]
  transfers between devices with their start and end apart: 1 -> 2, of which waited for: 1 -> 1; matrix products, arithmetic and copies ran while one was open for 0% -> 0% of each run, Pallas kernels for 1% -> 3%
where the time goes in v3:
time: 58 us; the launch traced here: 57.8 us
  blocking collectives  43.1 us (74%)
  Pallas kernels  11.6 us (20%)
  starting transfers between devices  1.59 us (3%)
  waiting for transfers between devices  0.91 us (2%)
    all_to_all x1, blocking collectives, per_device(): lax.all_to_all(summed, ('tm', 'nrn'), 0, 0, tiled=True, axis_index_groups...  24.9 us
    all_to_all x1, blocking collectives, per_device(): lax.all_to_all(mixed.reshape(devices, rows // devices, LANES), ('tm', 'nr...  18.2 us
    pallas_call x1, Pallas kernels, project(): pl.pallas_call(lambda *refs: project_kernel(*refs, pieces=pieces), out_sh...  7.27 us
    ppermute x2, starting transfers between devices, per_device(): lax.ppermute(x, 'nrn', [(j, j ^ 1) for j in range(neuron_groups)])  1.59 us
    pallas_call x1, Pallas kernels, project(): pl.pallas_call(rest_kernel, out_shape=(part(tail), part(tail)), compiler_...  1.39 us
    pallas_call x1, Pallas kernels, per_device(): pl.pallas_call(mlp_kernel, out_shape=jax.ShapeDtypeStruct((rows * LANES /...  1.33 us
  transfers between devices with their start and end apart: 2, of which 1 were waited for; matrix products, arithmetic and copies ran while one was open for 0% of the time, Pallas kernels for 3%

profile of v3, /device:TPU:1, one launch (start us, length us, event | category | flops | bytes accessed | tf_op | source)
XLA Modules:
  0.0 57.8 jit_solution(11378092763725665490)
XLA Ops:
  0.0 0.0 copy-start
  0.0 0.0 copy-start.1
  0.0 0.0 copy-start.4
  0.0 0.0 copy-start.5
  0.0 0.0 copy-start.2
  0.0 0.0 copy-start.3
  0.0 0.0 copy-start.12
  0.1 0.0 copy-start.13
  0.1 0.0 copy-start.6
  0.1 0.0 copy-start.7
  0.1 0.0 copy-start.11
  0.1 0.0 copy-start.14
  0.1 0.0 copy-start.8
  0.1 0.0 copy-start.9
  0.1 0.0 copy-start.10
  0.2 7.3 %project.1 = (f32[64,24,128]{2,1,0:T(8,128)S(1)}, f32[64,24,128]{2,1,0:T(8,128)S(1)}, bf16[1024,2048]{1,0:T(8,128)(2,1)S(1)}, bf16[2048,128]{1,0:T(8,128)(2,1)S(1)}) custom-call(s32[1]{0:T(128)} %bitcast.refs_0_, bf16[4096,2048]{1,0:T(8,128)(2,1)} %refs_1_.2, bf16[2048,128]{1,0:T(8,128)(2,1)} %refs_2_.3), custom_call_target="tpu_custom_call" | custom-call | tf_op jit(solution)/shard_map/project/pallas_call | solution.py:134
  7.4 1.5 %collective-permute-start = (f32[64,24,128]{2,1,0:T(8,128)S(1)}, f32[64,24,128]{2,1,0:T(8,128)S(1)}, u32[]{:S(2)}, u32[]{:S(2)}) collective-permute-start(f32[64,24,128]{2,1,0:T(8,128)S(1)} %get-tuple-element.14), channel_id=1, source_target_pairs={{0,1},{1,0},{2,3},{3,2},{4,5},{5,4},{6,7},{7,6},{8,9},{9,8},{10,11... | collective-permute-start | bytes 2359304 | tf_op jit(solution)/shard_map/ppermute | solution.py:223
  8.9 1.4 %rest.1 = (f32[64,8,128]{2,1,0:T(8,128)S(1)}, f32[64,8,128]{2,1,0:T(8,128)S(1)}) custom-call(bf16[1024,2048]{1,0:T(8,128)(2,1)S(1)} %get-tuple-element.15.rest_ref, bf16[2048,128]{1,0:T(8,128)(2,1)S(1)} %get-tuple-element.16.weight_ref), custom_call_target="tpu_custom_call" | custom-call | tf_op jit(solution)/shard_map/rest/pallas_call | solution.py:158
  10.3 0.1 collective-permute-start.1
  10.4 0.0 copy-done
  10.4 0.0 copy-done.1
  10.4 0.0 copy-done.4
  10.5 0.0 copy-done.5
  10.5 0.0 copy-done.2
  10.5 0.0 copy-done.3
  10.5 0.0 copy-done.11
  10.5 0.5 spectrum.1.refs_1_
  11.0 0.9 %collective-permute-done.1 = f32[64,8,128]{2,1,0:T(8,128)S(1)} collective-permute-done((f32[64,8,128]{2,1,0:T(8,128)S(1)}, f32[64,8,128]{2,1,0:T(8,128)S(1)}, u32[]{:S(2)}, u32[]{:S(2)}) %collective-permute-start.1) | collective-permute-done | bytes 262176 | tf_op jit(solution)/shard_map/ppermute | solution.py:223
  12.0 0.0 collective-permute-done
  12.0 0.1 add.11
  12.1 0.1 pad_maximum_fusion
  12.2 24.9 %all_to_all.10.refs_0_ = f32[64,32,128]{2,1,0:T(8,128)S(1)} all-to-all(f32[64,32,128]{2,1,0:T(8,128)S(1)} %pad_maximum_fusion), channel_id=1, replica_groups={{126,124,122,120,118,116,114,112,110,108,106,104,102,100,98,96,94,92,90..., dimensions={0} | all-to-all | bytes 2097152 | tf_op jit(solution)/shard_map/all_to_all | solution.py:234
  37.1 0.0 copy-done.12
  37.1 0.0 copy-done.13
  37.1 0.0 copy-done.6
  37.1 0.0 copy-done.7
  37.1 1.1 %convolve.1 = f32[256,128]{1,0:T(8,128)S(1)} custom-call(f32[64,32,128]{2,1,0:T(8,128)S(1)} %all_to_all.10.refs_0_, f32[136,256]{1,0:T(8,128)S(1)} %spectrum.1.refs_1_, bf16[272,256]{1,0:T(8,128)(2,1)S(1)} %copy-done, bf16[272,256]{1,0:T(8,128)(2,1)S(1)} %copy-done.1, f32[136,128]{1,0:T(8,128)S(1)} %copy-done.4, f32[136,128]{1,0:T(8,128)S(1)} %copy-done.5, ...), custom_call_target="tpu_custom_call" | custom-call | tf_op jit(solution)/shard_map/convolve/pallas_call | solution.py:235
  38.2 18.2 %all_to_all.11 = f32[128,2,128]{2,1,0:T(2,128)S(1)} all-to-all(f32[128,2,128]{2,1,0:T(2,128)S(1)} %bitcast.6), channel_id=1, replica_groups=mesh['tm'=8,'nrn'=16] {'tm','nrn'}, dimensions={0} | all-to-all | bytes 262144 | tf_op jit(solution)/shard_map/all_to_all | solution.py:241
  56.4 0.0 copy-done.14
  56.4 0.0 copy-done.8
  56.5 0.0 copy-done.9
  56.5 0.0 copy-done.10
  56.5 1.3 %mlp.1 = bf16[256,128]{1,0:T(8,128)(2,1)} custom-call(f32[256,128]{1,0:T(8,128)S(1)} %bitcast.5, f32[1,128]{1,0:T(1,128)S(1)} %bitcast.8, bf16[128,512]{1,0:T(8,128)(2,1)S(1)} %copy-done.8, bf16[128,512]{1,0:T(8,128)(2,1)S(1)} %copy-done.9, bf16[512,128]{1,0:T(8,128)(2,1)S(1)} %copy-done.10), custom_call_target="tpu_custom_call" | custom-call | tf_op jit(solution)/shard_map/mlp/pallas_call | solution.py:244
  (1 shorter events, 0.0 us)
Async XLA Ops:
  0.0 10.4 %copy-start = (bf16[272,256]{1,0:T(8,128)(2,1)S(1)}, bf16[272,256]{1,0:T(8,128)(2,1)}, u32[]{:S(2)}) copy-start(bf16[272,256]{1,0:T(8,128)(2,1)} %constant.39.clone.refs_1_.refs_2_) | copy-start | bytes 417796
  0.0 10.4 %copy-start.1 = (bf16[272,256]{1,0:T(8,128)(2,1)S(1)}, bf16[272,256]{1,0:T(8,128)(2,1)}, u32[]{:S(2)}) copy-start(bf16[272,256]{1,0:T(8,128)(2,1)} %constant.40.clone.refs_2_.refs_3_) | copy-start | bytes 417796
  0.0 10.4 %copy-start.4 = (f32[136,128]{1,0:T(8,128)S(1)}, f32[136,128]{1,0:T(8,128)}, u32[]{:S(2)}) copy-start(f32[136,128]{1,0:T(8,128)} %constant.37.clone.refs_3_.refs_4_) | copy-start | bytes 208900
  0.0 10.4 %copy-start.5 = (f32[136,128]{1,0:T(8,128)S(1)}, f32[136,128]{1,0:T(8,128)}, u32[]{:S(2)}) copy-start(f32[136,128]{1,0:T(8,128)} %constant.38.clone.refs_4_.refs_5_) | copy-start | bytes 208900
  0.0 10.4 %copy-start.2 = (bf16[256,256]{1,0:T(8,128)(2,1)S(1)}, bf16[256,256]{1,0:T(8,128)(2,1)}, u32[]{:S(2)}) copy-start(bf16[256,256]{1,0:T(8,128)(2,1)} %constant.41.clone.refs_5_.refs_6_) | copy-start | bytes 393220
  0.0 10.4 %copy-start.3 = (bf16[256,256]{1,0:T(8,128)(2,1)S(1)}, bf16[256,256]{1,0:T(8,128)(2,1)}, u32[]{:S(2)}) copy-start(bf16[256,256]{1,0:T(8,128)(2,1)} %constant.42.clone.refs_6_.refs_7_) | copy-start | bytes 393220
  0.0 37.1 %copy-start.12 = (bf16[256,256]{1,0:T(8,128)(2,1)S(1)}, bf16[256,256]{1,0:T(8,128)(2,1)}, u32[]{:S(2)}) copy-start(bf16[256,256]{1,0:T(8,128)(2,1)} %constant.43.clone.refs_8_) | copy-start | bytes 393220
  0.1 37.1 %copy-start.13 = (bf16[256,256]{1,0:T(8,128)(2,1)S(1)}, bf16[256,256]{1,0:T(8,128)(2,1)}, u32[]{:S(2)}) copy-start(bf16[256,256]{1,0:T(8,128)(2,1)} %constant.44.clone.refs_9_) | copy-start | bytes 393220
  0.1 37.1 %copy-start.6 = (bf16[256,272]{1,0:T(8,128)(2,1)S(1)}, bf16[256,272]{1,0:T(8,128)(2,1)}, u32[]{:S(2)}) copy-start(bf16[256,272]{1,0:T(8,128)(2,1)} %constant.45.clone.refs_10_) | copy-start | bytes 417796
  0.1 37.0 %copy-start.7 = (bf16[256,272]{1,0:T(8,128)(2,1)S(1)}, bf16[256,272]{1,0:T(8,128)(2,1)}, u32[]{:S(2)}) copy-start(bf16[256,272]{1,0:T(8,128)(2,1)} %constant.46.clone.refs_11_) | copy-start | bytes 417796
  0.1 10.4 %copy-start.11 = (f32[1,32768]{1,0:T(1,128)S(1)}, f32[1,32768]{1,0:T(1,128)}, u32[]{:S(2)}) copy-start(f32[1,32768]{1,0:T(1,128)} %param.19) | copy-start | bytes 393220
  0.1 56.3 %copy-start.14 = (f32[128]{0:T(128)S(1)}, f32[128]{0:T(128)}, u32[]{:S(2)}) copy-start(f32[128]{0:T(128)} %param.20) | copy-start | bytes 1540
  0.1 56.3 %copy-start.8 = (bf16[128,512]{1,0:T(8,128)(2,1)S(1)}, bf16[128,512]{1,0:T(8,128)(2,1)}, u32[]{:S(2)}) copy-start(bf16[128,512]{1,0:T(8,128)(2,1)} %gate_ref.1) | copy-start | bytes 393220
  0.1 56.3 %copy-start.9 = (bf16[128,512]{1,0:T(8,128)(2,1)S(1)}, bf16[128,512]{1,0:T(8,128)(2,1)}, u32[]{:S(2)}) copy-start(bf16[128,512]{1,0:T(8,128)(2,1)} %up_ref.1) | copy-start | bytes 393220
  0.1 56.3 %copy-start.10 = (bf16[512,128]{1,0:T(8,128)(2,1)S(1)}, bf16[512,128]{1,0:T(8,128)(2,1)}, u32[]{:S(2)}) copy-start(bf16[512,128]{1,0:T(8,128)(2,1)} %down_ref.1) | copy-start | bytes 393220
  7.4 4.5 %collective-permute-start = (f32[64,24,128]{2,1,0:T(8,128)S(1)}, f32[64,24,128]{2,1,0:T(8,128)S(1)}, u32[]{:S(2)}, u32[]{:S(2)}) collective-permute-start(f32[64,24,128]{2,1,0:T(8,128)S(1)} %get-tuple-element.14), channel_id=1, source_target_pairs={{0,1},{1,0},{2,3},{3,2},{4,5},{5,4},{6,7},{7,6},{8,9},{9,8},{10,11... | collective-permute-start | bytes 2359304 | tf_op jit(solution)/shard_map/ppermute | solution.py:223
  10.3 1.6 %collective-permute-start.1 = (f32[64,8,128]{2,1,0:T(8,128)S(1)}, f32[64,8,128]{2,1,0:T(8,128)S(1)}, u32[]{:S(2)}, u32[]{:S(2)}) collective-permute-start(f32[64,8,128]{2,1,0:T(8,128)S(1)} %get-tuple-element.18), channel_id=1, source_target_pairs={{0,1},{1,0},{2,3},{3,2},{4,5},{5,4},{6,7},{7,6},{8,9},{9,8},{10,11... | collective-permute-start | bytes 786440 | tf_op jit(solution)/shard_map/ppermute | solution.py:223

commit v4 on v3

--- a/solution.py
+++ b/solution.py
@@ -96,8 +96,8 @@
             spikes_hbm.at[pl.ds(starts[-1], rest_ref.shape[0])], rest_ref, arrived.at[len(pieces)]
         )
     )
-    for fetch in fetches[:2]:
-        fetch.start()
+    for i, fetch in enumerate(fetches[:3]):
+        fetch.start(priority=min(i, 1))
     fetch_read.wait()
     channel = lax.broadcasted_iota(jnp.int32, (width, width), 0)
     place = lax.broadcasted_iota(jnp.int32, (width, width), 1)
@@ -109,8 +109,8 @@
     held = None
     for i, (first, size) in enumerate(zip(starts, pieces)):
         fetches[i].wait()
-        if i + 2 < len(fetches):
-            fetches[i + 2].start()
+        if i + 3 < len(fetches):
+            fetches[i + 3].start(priority=1)
         rows = range(first, first + size, LANES)
         held = products(spikes_ref, weight_ref, rows, own_ref, other_ref, held)
     put(held[0], own_ref, other_ref, held[1])
@@ -229,7 +229,7 @@
         name="spectrum",
     )(kernel.reshape(rows, LANES), *ahead)
     swapped_rest, spec = lax.optimization_barrier((swapped_rest, spec))
-    summed = jnp.concatenate([own + swapped, own_rest + swapped_rest], axis=1)
+    summed = jnp.concatenate([own, own_rest], axis=1) + jnp.concatenate([swapped, swapped_rest], axis=1)
     same = [[d for d in range(devices) if d % 2 == c][::-1] for c in range(2)]
     parts = lax.all_to_all(summed, ("tm", "nrn"), 0, 0, tiled=True, axis_index_groups=same)
     mixed = pl.pallas_call(

time: 58 us -> 57.4 us (0.990)
  no operation moved by 1% of the time
where the time goes in v4:
time: 57.4 us; the launch traced here: 57.2 us
  blocking collectives  43.2 us (75%)
  Pallas kernels  11.1 us (19%)
  starting transfers between devices  1.55 us (3%)
  waiting for transfers between devices  0.91 us (2%)
    all_to_all x1, blocking collectives, per_device(): lax.all_to_all(summed, ('tm', 'nrn'), 0, 0, tiled=True, axis_index_groups...  25 us
    all_to_all x1, blocking collectives, per_device(): lax.all_to_all(mixed.reshape(devices, rows // devices, LANES), ('tm', 'nr...  18.2 us
    pallas_call x1, Pallas kernels, project(): pl.pallas_call(lambda *refs: project_kernel(*refs, pieces=pieces), out_sh...  6.81 us
    ppermute x2, starting transfers between devices, per_device(): lax.ppermute(x, 'nrn', [(j, j ^ 1) for j in range(neuron_groups)])  1.55 us
    pallas_call x1, Pallas kernels, project(): pl.pallas_call(rest_kernel, out_shape=(part(tail), part(tail)), compiler_...  1.39 us
    pallas_call x1, Pallas kernels, per_device(): pl.pallas_call(mlp_kernel, out_shape=jax.ShapeDtypeStruct((rows * LANES /...  1.32 us
  transfers between devices with their start and end apart: 2, of which 1 were waited for; matrix products, arithmetic and copies ran while one was open for 0% of the time, Pallas kernels for 3%

profile of v4, /device:TPU:1, one launch (start us, length us, event | category | flops | bytes accessed | tf_op | source)
XLA Modules:
  0.0 57.2 jit_solution(15750740288654822105)
XLA Ops:
  0.0 0.0 copy-start.4
  0.0 0.0 copy-start.5
  0.0 0.0 copy-start
  0.0 0.0 copy-start.1
  0.0 0.0 copy-start.2
  0.0 0.0 copy-start.3
  0.0 0.0 copy-start.12
  0.1 0.0 copy-start.13
  0.1 0.0 copy-start.6
  0.1 0.0 copy-start.7
  0.1 0.0 copy-start.11
  0.1 0.0 copy-start.14
  0.1 0.0 copy-start.8
  0.1 0.0 copy-start.9
  0.1 0.0 copy-start.10
  0.2 6.8 %project.1 = (f32[64,24,128]{2,1,0:T(8,128)S(1)}, f32[64,24,128]{2,1,0:T(8,128)S(1)}, bf16[1024,2048]{1,0:T(8,128)(2,1)S(1)}, bf16[2048,128]{1,0:T(8,128)(2,1)S(1)}) custom-call(s32[1]{0:T(128)} %bitcast.refs_0_, bf16[4096,2048]{1,0:T(8,128)(2,1)} %refs_1_.2, bf16[2048,128]{1,0:T(8,128)(2,1)} %refs_2_.3), custom_call_target="tpu_custom_call" | custom-call | tf_op jit(solution)/shard_map/project/pallas_call | solution.py:134
  7.0 1.5 %collective-permute-start = (f32[64,24,128]{2,1,0:T(8,128)S(1)}, f32[64,24,128]{2,1,0:T(8,128)S(1)}, u32[]{:S(2)}, u32[]{:S(2)}) collective-permute-start(f32[64,24,128]{2,1,0:T(8,128)S(1)} %get-tuple-element.17), channel_id=1, source_target_pairs={{0,1},{1,0},{2,3},{3,2},{4,5},{5,4},{6,7},{7,6},{8,9},{9,8},{10,11... | collective-permute-start | bytes 2359304 | tf_op jit(solution)/shard_map/ppermute | solution.py:223
  8.4 1.4 %rest.1 = (f32[64,8,128]{2,1,0:T(8,128)S(1)}, f32[64,8,128]{2,1,0:T(8,128)S(1)}) custom-call(bf16[1024,2048]{1,0:T(8,128)(2,1)S(1)} %get-tuple-element.14.rest_ref, bf16[2048,128]{1,0:T(8,128)(2,1)S(1)} %get-tuple-element.15.weight_ref), custom_call_target="tpu_custom_call" | custom-call | tf_op jit(solution)/shard_map/rest/pallas_call | solution.py:158
  9.8 0.1 collective-permute-start.1
  9.9 0.0 copy-done.4
  9.9 0.0 copy-done.5
  9.9 0.0 copy-done
  10.0 0.0 copy-done.1
  10.0 0.0 copy-done.2
  10.0 0.0 copy-done.3
  10.0 0.0 copy-done.11
  10.0 0.5 spectrum.1.refs_1_
  10.5 0.9 %collective-permute-done.1 = f32[64,8,128]{2,1,0:T(8,128)S(1)} collective-permute-done((f32[64,8,128]{2,1,0:T(8,128)S(1)}, f32[64,8,128]{2,1,0:T(8,128)S(1)}, u32[]{:S(2)}, u32[]{:S(2)}) %collective-permute-start.1) | collective-permute-done | bytes 262176 | tf_op jit(solution)/shard_map/ppermute | solution.py:223
  11.5 0.0 collective-permute-done
  11.5 0.1 maximum_add_fusion
  11.6 25.0 %all_to_all.10.refs_0_ = f32[64,32,128]{2,1,0:T(8,128)S(1)} all-to-all(f32[64,32,128]{2,1,0:T(8,128)S(1)} %maximum_add_fusion), channel_id=1, replica_groups={{126,124,122,120,118,116,114,112,110,108,106,104,102,100,98,96,94,92,90..., dimensions={0} | all-to-all | bytes 2097152 | tf_op jit(solution)/shard_map/all_to_all | solution.py:234
  36.6 0.0 copy-done.12
  36.6 0.0 copy-done.13
  36.6 0.0 copy-done.6
  36.6 0.0 copy-done.7
  36.6 1.1 %convolve.1 = f32[256,128]{1,0:T(8,128)S(1)} custom-call(f32[64,32,128]{2,1,0:T(8,128)S(1)} %all_to_all.10.refs_0_, f32[136,256]{1,0:T(8,128)S(1)} %spectrum.1.refs_1_, bf16[272,256]{1,0:T(8,128)(2,1)S(1)} %copy-done, bf16[272,256]{1,0:T(8,128)(2,1)S(1)} %copy-done.1, f32[136,128]{1,0:T(8,128)S(1)} %copy-done.4, f32[136,128]{1,0:T(8,128)S(1)} %copy-done.5, ...), custom_call_target="tpu_custom_call" | custom-call | tf_op jit(solution)/shard_map/convolve/pallas_call | solution.py:235
  37.7 18.2 %all_to_all.11 = f32[128,2,128]{2,1,0:T(2,128)S(1)} all-to-all(f32[128,2,128]{2,1,0:T(2,128)S(1)} %bitcast.6), channel_id=1, replica_groups=mesh['tm'=8,'nrn'=16] {'tm','nrn'}, dimensions={0} | all-to-all | bytes 262144 | tf_op jit(solution)/shard_map/all_to_all | solution.py:241
  55.9 0.0 copy-done.14
  55.9 0.0 copy-done.8
  55.9 0.0 copy-done.9
  55.9 0.0 copy-done.10
  55.9 1.3 %mlp.1 = bf16[256,128]{1,0:T(8,128)(2,1)} custom-call(f32[256,128]{1,0:T(8,128)S(1)} %bitcast.5, f32[1,128]{1,0:T(1,128)S(1)} %bitcast.8, bf16[128,512]{1,0:T(8,128)(2,1)S(1)} %copy-done.8, bf16[128,512]{1,0:T(8,128)(2,1)S(1)} %copy-done.9, bf16[512,128]{1,0:T(8,128)(2,1)S(1)} %copy-done.10), custom_call_target="tpu_custom_call" | custom-call | tf_op jit(solution)/shard_map/mlp/pallas_call | solution.py:244
Async XLA Ops:
  0.0 9.9 %copy-start.4 = (f32[136,128]{1,0:T(8,128)S(1)}, f32[136,128]{1,0:T(8,128)}, u32[]{:S(2)}) copy-start(f32[136,128]{1,0:T(8,128)} %constant.37.clone.refs_3_.refs_4_) | copy-start | bytes 208900
  0.0 9.9 %copy-start.5 = (f32[136,128]{1,0:T(8,128)S(1)}, f32[136,128]{1,0:T(8,128)}, u32[]{:S(2)}) copy-start(f32[136,128]{1,0:T(8,128)} %constant.38.clone.refs_4_.refs_5_) | copy-start | bytes 208900
  0.0 9.9 %copy-start = (bf16[272,256]{1,0:T(8,128)(2,1)S(1)}, bf16[272,256]{1,0:T(8,128)(2,1)}, u32[]{:S(2)}) copy-start(bf16[272,256]{1,0:T(8,128)(2,1)} %constant.39.clone.refs_1_.refs_2_) | copy-start | bytes 417796
  0.0 10.0 %copy-start.1 = (bf16[272,256]{1,0:T(8,128)(2,1)S(1)}, bf16[272,256]{1,0:T(8,128)(2,1)}, u32[]{:S(2)}) copy-start(bf16[272,256]{1,0:T(8,128)(2,1)} %constant.40.clone.refs_2_.refs_3_) | copy-start | bytes 417796
  0.0 9.9 %copy-start.2 = (bf16[256,256]{1,0:T(8,128)(2,1)S(1)}, bf16[256,256]{1,0:T(8,128)(2,1)}, u32[]{:S(2)}) copy-start(bf16[256,256]{1,0:T(8,128)(2,1)} %constant.41.clone.refs_5_.refs_6_) | copy-start | bytes 393220
  0.0 9.9 %copy-start.3 = (bf16[256,256]{1,0:T(8,128)(2,1)S(1)}, bf16[256,256]{1,0:T(8,128)(2,1)}, u32[]{:S(2)}) copy-start(bf16[256,256]{1,0:T(8,128)(2,1)} %constant.42.clone.refs_6_.refs_7_) | copy-start | bytes 393220
  0.0 36.5 %copy-start.12 = (bf16[256,256]{1,0:T(8,128)(2,1)S(1)}, bf16[256,256]{1,0:T(8,128)(2,1)}, u32[]{:S(2)}) copy-start(bf16[256,256]{1,0:T(8,128)(2,1)} %constant.43.clone.refs_8_) | copy-start | bytes 393220
  0.1 36.5 %copy-start.13 = (bf16[256,256]{1,0:T(8,128)(2,1)S(1)}, bf16[256,256]{1,0:T(8,128)(2,1)}, u32[]{:S(2)}) copy-start(bf16[256,256]{1,0:T(8,128)(2,1)} %constant.44.clone.refs_9_) | copy-start | bytes 393220
  0.1 36.5 %copy-start.6 = (bf16[256,272]{1,0:T(8,128)(2,1)S(1)}, bf16[256,272]{1,0:T(8,128)(2,1)}, u32[]{:S(2)}) copy-start(bf16[256,272]{1,0:T(8,128)(2,1)} %constant.45.clone.refs_10_) | copy-start | bytes 417796
  0.1 36.5 %copy-start.7 = (bf16[256,272]{1,0:T(8,128)(2,1)S(1)}, bf16[256,272]{1,0:T(8,128)(2,1)}, u32[]{:S(2)}) copy-start(bf16[256,272]{1,0:T(8,128)(2,1)} %constant.46.clone.refs_11_) | copy-start | bytes 417796
  0.1 9.9 %copy-start.11 = (f32[1,32768]{1,0:T(1,128)S(1)}, f32[1,32768]{1,0:T(1,128)}, u32[]{:S(2)}) copy-start(f32[1,32768]{1,0:T(1,128)} %param.19) | copy-start | bytes 393220
  0.1 55.8 %copy-start.14 = (f32[128]{0:T(128)S(1)}, f32[128]{0:T(128)}, u32[]{:S(2)}) copy-start(f32[128]{0:T(128)} %param.20) | copy-start | bytes 1540
  0.1 55.8 %copy-start.8 = (bf16[128,512]{1,0:T(8,128)(2,1)S(1)}, bf16[128,512]{1,0:T(8,128)(2,1)}, u32[]{:S(2)}) copy-start(bf16[128,512]{1,0:T(8,128)(2,1)} %gate_ref.1) | copy-start | bytes 393220
  0.1 55.8 %copy-start.9 = (bf16[128,512]{1,0:T(8,128)(2,1)S(1)}, bf16[128,512]{1,0:T(8,128)(2,1)}, u32[]{:S(2)}) copy-start(bf16[128,512]{1,0:T(8,128)(2,1)} %up_ref.1) | copy-start | bytes 393220
  0.1 55.8 %copy-start.10 = (bf16[512,128]{1,0:T(8,128)(2,1)S(1)}, bf16[512,128]{1,0:T(8,128)(2,1)}, u32[]{:S(2)}) copy-start(bf16[512,128]{1,0:T(8,128)(2,1)} %down_ref.1) | copy-start | bytes 393220
  7.0 4.5 %collective-permute-start = (f32[64,24,128]{2,1,0:T(8,128)S(1)}, f32[64,24,128]{2,1,0:T(8,128)S(1)}, u32[]{:S(2)}, u32[]{:S(2)}) collective-permute-start(f32[64,24,128]{2,1,0:T(8,128)S(1)} %get-tuple-element.17), channel_id=1, source_target_pairs={{0,1},{1,0},{2,3},{3,2},{4,5},{5,4},{6,7},{7,6},{8,9},{9,8},{10,11... | collective-permute-start | bytes 2359304 | tf_op jit(solution)/shard_map/ppermute | solution.py:223
  9.8 1.6 %collective-permute-start.1 = (f32[64,8,128]{2,1,0:T(8,128)S(1)}, f32[64,8,128]{2,1,0:T(8,128)S(1)}, u32[]{:S(2)}, u32[]{:S(2)}) collective-permute-start(f32[64,8,128]{2,1,0:T(8,128)S(1)} %get-tuple-element.18), channel_id=1, source_target_pairs={{0,1},{1,0},{2,3},{3,2},{4,5},{5,4},{6,7},{7,6},{8,9},{9,8},{10,11... | collective-permute-start | bytes 786440 | tf_op jit(solution)/shard_map/ppermute | solution.py:223

commit v5 on v4

--- a/solution.py
+++ b/solution.py
@@ -78,7 +78,7 @@
     return held
 
 
-def project_kernel(core_ref, spikes_hbm, read_hbm, own_ref, other_ref, rest_ref, weight_ref, *scratch, pieces):
+def project_kernel(core_ref, spikes_hbm, read_hbm, own_ref, other_ref, rest_ref, weight_ref, *scratch, pieces, torus):
     spikes_ref, read_ref, arrived, read_arrived = scratch
     width = read_ref.shape[1]
     half = width // 2
@@ -103,7 +103,10 @@
     place = lax.broadcasted_iota(jnp.int32, (width, width), 1)
     late = (place >= half).astype(jnp.int32)
     core = core_ref[0]
-    wanted = 2 * (half - 1 - (place - half * late)) + (core + late - 2 * core * late)
+    chip = half - 1 - (place - half * late)
+    ys, xs, zs = torus
+    chip = chip % ys * (xs * zs) + chip // (zs * ys) * zs + chip // ys % zs
+    wanted = 2 * chip + (core + late - 2 * core * late)
     pick = jnp.where(channel == wanted, 1.0, 0.0).astype(bf16)
     weight_ref[...] = jnp.dot(read_ref[...], pick, preferred_element_type=f32).astype(bf16)
     held = None
@@ -123,7 +126,7 @@
     put(held[0], own_ref, other_ref, held[1])
 
 
-def project(core, spikes, read_in, swap):
+def project(core, spikes, read_in, swap, torus):
     bins, neurons = spikes.shape
     width = read_in.shape[1]
     part = lambda rows: jax.ShapeDtypeStruct((width // 2, rows // LANES, LANES), f32)
@@ -132,7 +135,7 @@
     tail = bins - head
     vmem = pl.BlockSpec(memory_space=pltpu.VMEM)
     own, other, rest, weight = pl.pallas_call(
-        lambda *refs: project_kernel(*refs, pieces=pieces),
+        lambda *refs: project_kernel(*refs, pieces=pieces, torus=torus),
         out_shape=(
             part(head),
             part(head),
@@ -169,16 +172,21 @@
 
 
 def convolve_kernel(
-    parts_ref, spec_ref, fh, fl, tc, ts, sh, sl, th, tl, gh, gl, out_ref, *, padded, groups
+    parts_ref, spec_ref, fh, fl, tc, ts, sh, sl, th, tl, gh, gl, out_ref, *, padded, split_tm, split_nrn
 ):
-    parts = parts_ref[...]
-    each, lanes = parts.shape[1], parts.shape[2]
-    members = parts.shape[0] // groups
-    parts = parts.reshape(groups, members, each, lanes)
-    series = parts[:, 0]
-    for m in range(1, members):
-        series = series + parts[:, m]
-    series = jnp.concatenate([series[g] for g in reversed(range(groups))], axis=0)
+    each, lanes = parts_ref.shape[1:]
+    (ys, x_his), (x_los, zs) = split_tm, split_nrn
+    parts = parts_ref[...].reshape(x_his, x_los, zs, ys, each, lanes)
+    blocks = []
+    for y in range(ys):
+        for x_hi in range(x_his):
+            block = None
+            for x_lo in range(x_los):
+                for z in range(zs):
+                    part = parts[x_his - 1 - x_hi, x_los - 1 - x_lo, zs - 1 - z, ys - 1 - y]
+                    block = part if block is None else block + part
+            blocks.append(block)
+    series = jnp.concatenate(blocks, axis=0)
     data = forward(series, (fh, fl, tc, ts, sh, sl), padded)
     dr, di = data[:, :LANES], data[:, LANES:]
     spec = spec_ref[...]
@@ -221,7 +229,10 @@
         pltpu.with_memory_space_constraint(x, pltpu.HBM) for x in (spikes, read_in)
     )
     swap = lambda x: lax.ppermute(x, "nrn", [(j, j ^ 1) for j in range(neuron_groups)])
-    own, swapped, own_rest, swapped_rest = project(core, spikes, read_in, swap)
+    split_tm = (time_groups // 2, 2)
+    split_nrn = (2, neuron_groups // 4)
+    ys, xs, zs = split_tm[0], split_tm[1] * split_nrn[0], split_nrn[1]
+    own, swapped, own_rest, swapped_rest = project(core, spikes, read_in, swap, (ys, xs, zs))
     spec = pl.pallas_call(
         lambda *refs: spectrum_kernel(*refs, padded=padded, scale=1.0 / session),
         out_shape=jax.ShapeDtypeStruct((padded, 2 * LANES), f32),
@@ -230,10 +241,13 @@
     )(kernel.reshape(rows, LANES), *ahead)
     swapped_rest, spec = lax.optimization_barrier((swapped_rest, spec))
     summed = jnp.concatenate([own, own_rest], axis=1) + jnp.concatenate([swapped, swapped_rest], axis=1)
-    same = [[d for d in range(devices) if d % 2 == c][::-1] for c in range(2)]
+    chips = [(y * xs + x) * zs + z for x in range(xs) for z in range(zs) for y in range(ys)][::-1]
+    same = [[2 * chip + c for chip in chips] for c in range(2)]
     parts = lax.all_to_all(summed, ("tm", "nrn"), 0, 0, tiled=True, axis_index_groups=same)
     mixed = pl.pallas_call(
-        lambda *refs: convolve_kernel(*refs, padded=padded, groups=time_groups),
+        lambda *refs: convolve_kernel(
+            *refs, padded=padded, split_tm=split_tm, split_nrn=split_nrn
+        ),
         out_shape=jax.ShapeDtypeStruct((rows, LANES), f32),
         compiler_params=pltpu.CompilerParams(vmem_limit_bytes=12 << 20),
         name="convolve",

time: 57.4 us -> 57.2 us (level)
  no operation moved by 1% of the time
where the time goes in v5:
time: 57.2 us; the launch traced here: 57 us
  blocking collectives  43 us (75%)
  Pallas kernels  11.1 us (19%)
  starting transfers between devices  1.55 us (3%)
  waiting for transfers between devices  0.91 us (2%)
    all_to_all x1, blocking collectives, per_device(): lax.all_to_all(summed, ('tm', 'nrn'), 0, 0, tiled=True, axis_index_groups...  24.7 us
    all_to_all x1, blocking collectives, per_device(): lax.all_to_all(mixed.reshape(devices, rows // devices, LANES), ('tm', 'nr...  18.3 us
    pallas_call x1, Pallas kernels, project(): pl.pallas_call(lambda *refs: project_kernel(*refs, pieces=pieces, torus=t...  6.81 us
    ppermute x2, starting transfers between devices, per_device(): lax.ppermute(x, 'nrn', [(j, j ^ 1) for j in range(neuron_groups)])  1.55 us
    pallas_call x1, Pallas kernels, project(): pl.pallas_call(rest_kernel, out_shape=(part(tail), part(tail)), compiler_...  1.39 us
    pallas_call x1, Pallas kernels, per_device(): pl.pallas_call(mlp_kernel, out_shape=jax.ShapeDtypeStruct((rows * LANES /...  1.32 us
  transfers between devices with their start and end apart: 2, of which 1 were waited for; matrix products, arithmetic and copies ran while one was open for 0% of the time, Pallas kernels for 3%

profile of v5, /device:TPU:1, one launch (start us, length us, event | category | flops | bytes accessed | tf_op | source)
XLA Modules:
  0.0 57.0 jit_solution(13015619483447523488)
XLA Ops:
  0.0 0.0 copy-start.4
  0.0 0.0 copy-start.5
  0.0 0.0 copy-start
  0.0 0.0 copy-start.1
  0.0 0.0 copy-start.2
  0.0 0.0 copy-start.3
  0.0 0.0 copy-start.12
  0.1 0.0 copy-start.13
  0.1 0.0 copy-start.6
  0.1 0.0 copy-start.7
  0.1 0.0 copy-start.11
  0.1 0.0 copy-start.14
  0.1 0.0 copy-start.8
  0.1 0.0 copy-start.9
  0.1 0.0 copy-start.10
  0.2 6.8 %project.1 = (f32[64,24,128]{2,1,0:T(8,128)S(1)}, f32[64,24,128]{2,1,0:T(8,128)S(1)}, bf16[1024,2048]{1,0:T(8,128)(2,1)S(1)}, bf16[2048,128]{1,0:T(8,128)(2,1)S(1)}) custom-call(s32[1]{0:T(128)} %bitcast.refs_0_, bf16[4096,2048]{1,0:T(8,128)(2,1)} %refs_1_.2, bf16[2048,128]{1,0:T(8,128)(2,1)} %refs_2_.3), custom_call_target="tpu_custom_call" | custom-call | tf_op jit(solution)/shard_map/project/pallas_call | solution.py:137
  7.0 1.5 %collective-permute-start = (f32[64,24,128]{2,1,0:T(8,128)S(1)}, f32[64,24,128]{2,1,0:T(8,128)S(1)}, u32[]{:S(2)}, u32[]{:S(2)}) collective-permute-start(f32[64,24,128]{2,1,0:T(8,128)S(1)} %get-tuple-element.17), channel_id=1, source_target_pairs={{0,1},{1,0},{2,3},{3,2},{4,5},{5,4},{6,7},{7,6},{8,9},{9,8},{10,11... | collective-permute-start | bytes 2359304 | tf_op jit(solution)/shard_map/ppermute | solution.py:231
  8.4 1.4 %rest.1 = (f32[64,8,128]{2,1,0:T(8,128)S(1)}, f32[64,8,128]{2,1,0:T(8,128)S(1)}) custom-call(bf16[1024,2048]{1,0:T(8,128)(2,1)S(1)} %get-tuple-element.14.rest_ref, bf16[2048,128]{1,0:T(8,128)(2,1)S(1)} %get-tuple-element.15.weight_ref), custom_call_target="tpu_custom_call" | custom-call | tf_op jit(solution)/shard_map/rest/pallas_call | solution.py:161
  9.8 0.1 collective-permute-start.1
  9.9 0.0 copy-done.4
  9.9 0.0 copy-done.5
  9.9 0.0 copy-done
  10.0 0.0 copy-done.1
  10.0 0.0 copy-done.2
  10.0 0.0 copy-done.3
  10.0 0.0 copy-done.11
  10.0 0.5 spectrum.1.refs_1_
  10.5 0.9 %collective-permute-done.1 = f32[64,8,128]{2,1,0:T(8,128)S(1)} collective-permute-done((f32[64,8,128]{2,1,0:T(8,128)S(1)}, f32[64,8,128]{2,1,0:T(8,128)S(1)}, u32[]{:S(2)}, u32[]{:S(2)}) %collective-permute-start.1) | collective-permute-done | bytes 262176 | tf_op jit(solution)/shard_map/ppermute | solution.py:231
  11.5 0.0 collective-permute-done
  11.5 0.1 maximum_add_fusion
  11.6 24.7 %all_to_all.10.refs_0_ = f32[64,32,128]{2,1,0:T(8,128)S(1)} all-to-all(f32[64,32,128]{2,1,0:T(8,128)S(1)} %maximum_add_fusion), channel_id=1, replica_groups={{126,94,62,30,124,92,60,28,122,90,58,26,120,88,56,24,118,86,54,22,116,8..., dimensions={0} | all-to-all | bytes 2097152 | tf_op jit(solution)/shard_map/all_to_all | solution.py:246
  36.3 0.0 copy-done.12
  36.3 0.0 copy-done.13
  36.3 0.0 copy-done.6
  36.3 0.0 copy-done.7
  36.3 1.1 %convolve.1 = f32[256,128]{1,0:T(8,128)S(1)} custom-call(f32[64,32,128]{2,1,0:T(8,128)S(1)} %all_to_all.10.refs_0_, f32[136,256]{1,0:T(8,128)S(1)} %spectrum.1.refs_1_, bf16[272,256]{1,0:T(8,128)(2,1)S(1)} %copy-done, bf16[272,256]{1,0:T(8,128)(2,1)S(1)} %copy-done.1, f32[136,128]{1,0:T(8,128)S(1)} %copy-done.4, f32[136,128]{1,0:T(8,128)S(1)} %copy-done.5, ...), custom_call_target="tpu_custom_call" | custom-call | tf_op jit(solution)/shard_map/convolve/pallas_call | solution.py:247
  37.4 18.3 %all_to_all.11 = f32[128,2,128]{2,1,0:T(2,128)S(1)} all-to-all(f32[128,2,128]{2,1,0:T(2,128)S(1)} %bitcast.6), channel_id=1, replica_groups=mesh['tm'=8,'nrn'=16] {'tm','nrn'}, dimensions={0} | all-to-all | bytes 262144 | tf_op jit(solution)/shard_map/all_to_all | solution.py:255
  55.7 0.0 copy-done.14
  55.7 0.0 copy-done.8
  55.7 0.0 copy-done.9
  55.7 0.0 copy-done.10
  55.7 1.3 %mlp.1 = bf16[256,128]{1,0:T(8,128)(2,1)} custom-call(f32[256,128]{1,0:T(8,128)S(1)} %bitcast.5, f32[1,128]{1,0:T(1,128)S(1)} %bitcast.8, bf16[128,512]{1,0:T(8,128)(2,1)S(1)} %copy-done.8, bf16[128,512]{1,0:T(8,128)(2,1)S(1)} %copy-done.9, bf16[512,128]{1,0:T(8,128)(2,1)S(1)} %copy-done.10), custom_call_target="tpu_custom_call" | custom-call | tf_op jit(solution)/shard_map/mlp/pallas_call | solution.py:258
Async XLA Ops:
  0.0 9.9 %copy-start.4 = (f32[136,128]{1,0:T(8,128)S(1)}, f32[136,128]{1,0:T(8,128)}, u32[]{:S(2)}) copy-start(f32[136,128]{1,0:T(8,128)} %constant.37.clone.refs_3_.refs_4_) | copy-start | bytes 208900
  0.0 9.9 %copy-start.5 = (f32[136,128]{1,0:T(8,128)S(1)}, f32[136,128]{1,0:T(8,128)}, u32[]{:S(2)}) copy-start(f32[136,128]{1,0:T(8,128)} %constant.38.clone.refs_4_.refs_5_) | copy-start | bytes 208900
  0.0 9.9 %copy-start = (bf16[272,256]{1,0:T(8,128)(2,1)S(1)}, bf16[272,256]{1,0:T(8,128)(2,1)}, u32[]{:S(2)}) copy-start(bf16[272,256]{1,0:T(8,128)(2,1)} %constant.39.clone.refs_1_.refs_2_) | copy-start | bytes 417796
  0.0 10.0 %copy-start.1 = (bf16[272,256]{1,0:T(8,128)(2,1)S(1)}, bf16[272,256]{1,0:T(8,128)(2,1)}, u32[]{:S(2)}) copy-start(bf16[272,256]{1,0:T(8,128)(2,1)} %constant.40.clone.refs_2_.refs_3_) | copy-start | bytes 417796
  0.0 9.9 %copy-start.2 = (bf16[256,256]{1,0:T(8,128)(2,1)S(1)}, bf16[256,256]{1,0:T(8,128)(2,1)}, u32[]{:S(2)}) copy-start(bf16[256,256]{1,0:T(8,128)(2,1)} %constant.41.clone.refs_5_.refs_6_) | copy-start | bytes 393220
  0.0 9.9 %copy-start.3 = (bf16[256,256]{1,0:T(8,128)(2,1)S(1)}, bf16[256,256]{1,0:T(8,128)(2,1)}, u32[]{:S(2)}) copy-start(bf16[256,256]{1,0:T(8,128)(2,1)} %constant.42.clone.refs_6_.refs_7_) | copy-start | bytes 393220
  0.0 36.2 %copy-start.12 = (bf16[256,256]{1,0:T(8,128)(2,1)S(1)}, bf16[256,256]{1,0:T(8,128)(2,1)}, u32[]{:S(2)}) copy-start(bf16[256,256]{1,0:T(8,128)(2,1)} %constant.43.clone.refs_8_) | copy-start | bytes 393220
  0.1 36.2 %copy-start.13 = (bf16[256,256]{1,0:T(8,128)(2,1)S(1)}, bf16[256,256]{1,0:T(8,128)(2,1)}, u32[]{:S(2)}) copy-start(bf16[256,256]{1,0:T(8,128)(2,1)} %constant.44.clone.refs_9_) | copy-start | bytes 393220
  0.1 36.2 %copy-start.6 = (bf16[256,272]{1,0:T(8,128)(2,1)S(1)}, bf16[256,272]{1,0:T(8,128)(2,1)}, u32[]{:S(2)}) copy-start(bf16[256,272]{1,0:T(8,128)(2,1)} %constant.45.clone.refs_10_) | copy-start | bytes 417796
  0.1 36.2 %copy-start.7 = (bf16[256,272]{1,0:T(8,128)(2,1)S(1)}, bf16[256,272]{1,0:T(8,128)(2,1)}, u32[]{:S(2)}) copy-start(bf16[256,272]{1,0:T(8,128)(2,1)} %constant.46.clone.refs_11_) | copy-start | bytes 417796
  0.1 9.9 %copy-start.11 = (f32[1,32768]{1,0:T(1,128)S(1)}, f32[1,32768]{1,0:T(1,128)}, u32[]{:S(2)}) copy-start(f32[1,32768]{1,0:T(1,128)} %param.19) | copy-start | bytes 393220
  0.1 55.6 %copy-start.14 = (f32[128]{0:T(128)S(1)}, f32[128]{0:T(128)}, u32[]{:S(2)}) copy-start(f32[128]{0:T(128)} %param.20) | copy-start | bytes 1540
  0.1 55.6 %copy-start.8 = (bf16[128,512]{1,0:T(8,128)(2,1)S(1)}, bf16[128,512]{1,0:T(8,128)(2,1)}, u32[]{:S(2)}) copy-start(bf16[128,512]{1,0:T(8,128)(2,1)} %gate_ref.1) | copy-start | bytes 393220
  0.1 55.6 %copy-start.9 = (bf16[128,512]{1,0:T(8,128)(2,1)S(1)}, bf16[128,512]{1,0:T(8,128)(2,1)}, u32[]{:S(2)}) copy-start(bf16[128,512]{1,0:T(8,128)(2,1)} %up_ref.1) | copy-start | bytes 393220
  0.1 55.6 %copy-start.10 = (bf16[512,128]{1,0:T(8,128)(2,1)S(1)}, bf16[512,128]{1,0:T(8,128)(2,1)}, u32[]{:S(2)}) copy-start(bf16[512,128]{1,0:T(8,128)(2,1)} %down_ref.1) | copy-start | bytes 393220
  7.0 4.5 %collective-permute-start = (f32[64,24,128]{2,1,0:T(8,128)S(1)}, f32[64,24,128]{2,1,0:T(8,128)S(1)}, u32[]{:S(2)}, u32[]{:S(2)}) collective-permute-start(f32[64,24,128]{2,1,0:T(8,128)S(1)} %get-tuple-element.17), channel_id=1, source_target_pairs={{0,1},{1,0},{2,3},{3,2},{4,5},{5,4},{6,7},{7,6},{8,9},{9,8},{10,11... | collective-permute-start | bytes 2359304 | tf_op jit(solution)/shard_map/ppermute | solution.py:231
  9.8 1.6 %collective-permute-start.1 = (f32[64,8,128]{2,1,0:T(8,128)S(1)}, f32[64,8,128]{2,1,0:T(8,128)S(1)}, u32[]{:S(2)}, u32[]{:S(2)}) collective-permute-start(f32[64,8,128]{2,1,0:T(8,128)S(1)} %get-tuple-element.18), channel_id=1, source_target_pairs={{0,1},{1,0},{2,3},{3,2},{4,5},{5,4},{6,7},{7,6},{8,9},{9,8},{10,11... | collective-permute-start | bytes 786440 | tf_op jit(solution)/shard_map/ppermute | solution.py:231

commit v6 on v5

--- a/solution.py
+++ b/solution.py
@@ -96,7 +96,7 @@
             spikes_hbm.at[pl.ds(starts[-1], rest_ref.shape[0])], rest_ref, arrived.at[len(pieces)]
         )
     )
-    for i, fetch in enumerate(fetches[:3]):
+    for i, fetch in enumerate(fetches[:4]):
         fetch.start(priority=min(i, 1))
     fetch_read.wait()
     channel = lax.broadcasted_iota(jnp.int32, (width, width), 0)
@@ -112,8 +112,8 @@
     held = None
     for i, (first, size) in enumerate(zip(starts, pieces)):
         fetches[i].wait()
-        if i + 3 < len(fetches):
-            fetches[i + 3].start(priority=1)
+        if i + 4 < len(fetches):
+            fetches[i + 4].start(priority=1)
         rows = range(first, first + size, LANES)
         held = products(spikes_ref, weight_ref, rows, own_ref, other_ref, held)
     put(held[0], own_ref, other_ref, held[1])

time: 57.2 us -> 57.2 us (level)
  no operation moved by 1% of the time
where the time goes in v6:
time: 57.2 us; the launch traced here: 57 us
  blocking collectives  43 us (75%)
  Pallas kernels  11.1 us (19%)
  starting transfers between devices  1.55 us (3%)
  waiting for transfers between devices  0.91 us (2%)
    all_to_all x1, blocking collectives, per_device(): lax.all_to_all(summed, ('tm', 'nrn'), 0, 0, tiled=True, axis_index_groups...  24.7 us
    all_to_all x1, blocking collectives, per_device(): lax.all_to_all(mixed.reshape(devices, rows // devices, LANES), ('tm', 'nr...  18.3 us
    pallas_call x1, Pallas kernels, project(): pl.pallas_call(lambda *refs: project_kernel(*refs, pieces=pieces, torus=t...  6.81 us
    ppermute x2, starting transfers between devices, per_device(): lax.ppermute(x, 'nrn', [(j, j ^ 1) for j in range(neuron_groups)])  1.55 us
    pallas_call x1, Pallas kernels, project(): pl.pallas_call(rest_kernel, out_shape=(part(tail), part(tail)), compiler_...  1.39 us
    pallas_call x1, Pallas kernels, per_device(): pl.pallas_call(mlp_kernel, out_shape=jax.ShapeDtypeStruct((rows * LANES /...  1.32 us
  transfers between devices with their start and end apart: 2, of which 1 were waited for; matrix products, arithmetic and copies ran while one was open for 0% of the time, Pallas kernels for 3%

profile of v6, /device:TPU:1, one launch (start us, length us, event | category | flops | bytes accessed | tf_op | source)
XLA Modules:
  0.0 57.0 jit_solution(13784664708745357934)
XLA Ops:
  0.0 0.0 copy-start.4
  0.0 0.0 copy-start.5
  0.0 0.0 copy-start
  0.0 0.0 copy-start.1
  0.0 0.0 copy-start.2
  0.0 0.0 copy-start.3
  0.0 0.0 copy-start.12
  0.1 0.0 copy-start.13
  0.1 0.0 copy-start.6
  0.1 0.0 copy-start.7
  0.1 0.0 copy-start.11
  0.1 0.0 copy-start.14
  0.1 0.0 copy-start.8
  0.1 0.0 copy-start.9
  0.1 0.0 copy-start.10
  0.2 6.8 %project.1 = (f32[64,24,128]{2,1,0:T(8,128)S(1)}, f32[64,24,128]{2,1,0:T(8,128)S(1)}, bf16[1024,2048]{1,0:T(8,128)(2,1)S(1)}, bf16[2048,128]{1,0:T(8,128)(2,1)S(1)}) custom-call(s32[1]{0:T(128)} %bitcast.refs_0_, bf16[4096,2048]{1,0:T(8,128)(2,1)} %refs_1_.2, bf16[2048,128]{1,0:T(8,128)(2,1)} %refs_2_.3), custom_call_target="tpu_custom_call" | custom-call | tf_op jit(solution)/shard_map/project/pallas_call | solution.py:137
  7.0 1.5 %collective-permute-start = (f32[64,24,128]{2,1,0:T(8,128)S(1)}, f32[64,24,128]{2,1,0:T(8,128)S(1)}, u32[]{:S(2)}, u32[]{:S(2)}) collective-permute-start(f32[64,24,128]{2,1,0:T(8,128)S(1)} %get-tuple-element.17), channel_id=1, source_target_pairs={{0,1},{1,0},{2,3},{3,2},{4,5},{5,4},{6,7},{7,6},{8,9},{9,8},{10,11... | collective-permute-start | bytes 2359304 | tf_op jit(solution)/shard_map/ppermute | solution.py:231
  8.4 1.4 %rest.1 = (f32[64,8,128]{2,1,0:T(8,128)S(1)}, f32[64,8,128]{2,1,0:T(8,128)S(1)}) custom-call(bf16[1024,2048]{1,0:T(8,128)(2,1)S(1)} %get-tuple-element.14.rest_ref, bf16[2048,128]{1,0:T(8,128)(2,1)S(1)} %get-tuple-element.15.weight_ref), custom_call_target="tpu_custom_call" | custom-call | tf_op jit(solution)/shard_map/rest/pallas_call | solution.py:161
  9.8 0.1 collective-permute-start.1
  9.9 0.0 copy-done.4
  9.9 0.0 copy-done.5
  9.9 0.0 copy-done
  10.0 0.0 copy-done.1
  10.0 0.0 copy-done.2
  10.0 0.0 copy-done.3
  10.0 0.0 copy-done.11
  10.0 0.5 spectrum.1.refs_1_
  10.5 0.9 %collective-permute-done.1 = f32[64,8,128]{2,1,0:T(8,128)S(1)} collective-permute-done((f32[64,8,128]{2,1,0:T(8,128)S(1)}, f32[64,8,128]{2,1,0:T(8,128)S(1)}, u32[]{:S(2)}, u32[]{:S(2)}) %collective-permute-start.1) | collective-permute-done | bytes 262176 | tf_op jit(solution)/shard_map/ppermute | solution.py:231
  11.5 0.0 collective-permute-done
  11.5 0.1 maximum_add_fusion
  11.6 24.7 %all_to_all.10.refs_0_ = f32[64,32,128]{2,1,0:T(8,128)S(1)} all-to-all(f32[64,32,128]{2,1,0:T(8,128)S(1)} %maximum_add_fusion), channel_id=1, replica_groups={{126,94,62,30,124,92,60,28,122,90,58,26,120,88,56,24,118,86,54,22,116,8..., dimensions={0} | all-to-all | bytes 2097152 | tf_op jit(solution)/shard_map/all_to_all | solution.py:246
  36.3 0.0 copy-done.12
  36.3 0.0 copy-done.13
  36.3 0.0 copy-done.6
  36.3 0.0 copy-done.7
  36.3 1.1 %convolve.1 = f32[256,128]{1,0:T(8,128)S(1)} custom-call(f32[64,32,128]{2,1,0:T(8,128)S(1)} %all_to_all.10.refs_0_, f32[136,256]{1,0:T(8,128)S(1)} %spectrum.1.refs_1_, bf16[272,256]{1,0:T(8,128)(2,1)S(1)} %copy-done, bf16[272,256]{1,0:T(8,128)(2,1)S(1)} %copy-done.1, f32[136,128]{1,0:T(8,128)S(1)} %copy-done.4, f32[136,128]{1,0:T(8,128)S(1)} %copy-done.5, ...), custom_call_target="tpu_custom_call" | custom-call | tf_op jit(solution)/shard_map/convolve/pallas_call | solution.py:247
  37.4 18.3 %all_to_all.11 = f32[128,2,128]{2,1,0:T(2,128)S(1)} all-to-all(f32[128,2,128]{2,1,0:T(2,128)S(1)} %bitcast.6), channel_id=1, replica_groups=mesh['tm'=8,'nrn'=16] {'tm','nrn'}, dimensions={0} | all-to-all | bytes 262144 | tf_op jit(solution)/shard_map/all_to_all | solution.py:255
  55.7 0.0 copy-done.14
  55.7 0.0 copy-done.8
  55.7 0.0 copy-done.9
  55.7 0.0 copy-done.10
  55.7 1.3 %mlp.1 = bf16[256,128]{1,0:T(8,128)(2,1)} custom-call(f32[256,128]{1,0:T(8,128)S(1)} %bitcast.5, f32[1,128]{1,0:T(1,128)S(1)} %bitcast.8, bf16[128,512]{1,0:T(8,128)(2,1)S(1)} %copy-done.8, bf16[128,512]{1,0:T(8,128)(2,1)S(1)} %copy-done.9, bf16[512,128]{1,0:T(8,128)(2,1)S(1)} %copy-done.10), custom_call_target="tpu_custom_call" | custom-call | tf_op jit(solution)/shard_map/mlp/pallas_call | solution.py:258
Async XLA Ops:
  0.0 9.9 %copy-start.4 = (f32[136,128]{1,0:T(8,128)S(1)}, f32[136,128]{1,0:T(8,128)}, u32[]{:S(2)}) copy-start(f32[136,128]{1,0:T(8,128)} %constant.37.clone.refs_3_.refs_4_) | copy-start | bytes 208900
  0.0 9.9 %copy-start.5 = (f32[136,128]{1,0:T(8,128)S(1)}, f32[136,128]{1,0:T(8,128)}, u32[]{:S(2)}) copy-start(f32[136,128]{1,0:T(8,128)} %constant.38.clone.refs_4_.refs_5_) | copy-start | bytes 208900
  0.0 9.9 %copy-start = (bf16[272,256]{1,0:T(8,128)(2,1)S(1)}, bf16[272,256]{1,0:T(8,128)(2,1)}, u32[]{:S(2)}) copy-start(bf16[272,256]{1,0:T(8,128)(2,1)} %constant.39.clone.refs_1_.refs_2_) | copy-start | bytes 417796
  0.0 10.0 %copy-start.1 = (bf16[272,256]{1,0:T(8,128)(2,1)S(1)}, bf16[272,256]{1,0:T(8,128)(2,1)}, u32[]{:S(2)}) copy-start(bf16[272,256]{1,0:T(8,128)(2,1)} %constant.40.clone.refs_2_.refs_3_) | copy-start | bytes 417796
  0.0 9.9 %copy-start.2 = (bf16[256,256]{1,0:T(8,128)(2,1)S(1)}, bf16[256,256]{1,0:T(8,128)(2,1)}, u32[]{:S(2)}) copy-start(bf16[256,256]{1,0:T(8,128)(2,1)} %constant.41.clone.refs_5_.refs_6_) | copy-start | bytes 393220
  0.0 9.9 %copy-start.3 = (bf16[256,256]{1,0:T(8,128)(2,1)S(1)}, bf16[256,256]{1,0:T(8,128)(2,1)}, u32[]{:S(2)}) copy-start(bf16[256,256]{1,0:T(8,128)(2,1)} %constant.42.clone.refs_6_.refs_7_) | copy-start | bytes 393220
  0.0 36.2 %copy-start.12 = (bf16[256,256]{1,0:T(8,128)(2,1)S(1)}, bf16[256,256]{1,0:T(8,128)(2,1)}, u32[]{:S(2)}) copy-start(bf16[256,256]{1,0:T(8,128)(2,1)} %constant.43.clone.refs_8_) | copy-start | bytes 393220
  0.1 36.2 %copy-start.13 = (bf16[256,256]{1,0:T(8,128)(2,1)S(1)}, bf16[256,256]{1,0:T(8,128)(2,1)}, u32[]{:S(2)}) copy-start(bf16[256,256]{1,0:T(8,128)(2,1)} %constant.44.clone.refs_9_) | copy-start | bytes 393220
  0.1 36.2 %copy-start.6 = (bf16[256,272]{1,0:T(8,128)(2,1)S(1)}, bf16[256,272]{1,0:T(8,128)(2,1)}, u32[]{:S(2)}) copy-start(bf16[256,272]{1,0:T(8,128)(2,1)} %constant.45.clone.refs_10_) | copy-start | bytes 417796
  0.1 36.2 %copy-start.7 = (bf16[256,272]{1,0:T(8,128)(2,1)S(1)}, bf16[256,272]{1,0:T(8,128)(2,1)}, u32[]{:S(2)}) copy-start(bf16[256,272]{1,0:T(8,128)(2,1)} %constant.46.clone.refs_11_) | copy-start | bytes 417796
  0.1 9.9 %copy-start.11 = (f32[1,32768]{1,0:T(1,128)S(1)}, f32[1,32768]{1,0:T(1,128)}, u32[]{:S(2)}) copy-start(f32[1,32768]{1,0:T(1,128)} %param.19) | copy-start | bytes 393220
  0.1 55.6 %copy-start.14 = (f32[128]{0:T(128)S(1)}, f32[128]{0:T(128)}, u32[]{:S(2)}) copy-start(f32[128]{0:T(128)} %param.20) | copy-start | bytes 1540
  0.1 55.6 %copy-start.8 = (bf16[128,512]{1,0:T(8,128)(2,1)S(1)}, bf16[128,512]{1,0:T(8,128)(2,1)}, u32[]{:S(2)}) copy-start(bf16[128,512]{1,0:T(8,128)(2,1)} %gate_ref.1) | copy-start | bytes 393220
  0.1 55.6 %copy-start.9 = (bf16[128,512]{1,0:T(8,128)(2,1)S(1)}, bf16[128,512]{1,0:T(8,128)(2,1)}, u32[]{:S(2)}) copy-start(bf16[128,512]{1,0:T(8,128)(2,1)} %up_ref.1) | copy-start | bytes 393220
  0.1 55.6 %copy-start.10 = (bf16[512,128]{1,0:T(8,128)(2,1)S(1)}, bf16[512,128]{1,0:T(8,128)(2,1)}, u32[]{:S(2)}) copy-start(bf16[512,128]{1,0:T(8,128)(2,1)} %down_ref.1) | copy-start | bytes 393220
  7.0 4.5 %collective-permute-start = (f32[64,24,128]{2,1,0:T(8,128)S(1)}, f32[64,24,128]{2,1,0:T(8,128)S(1)}, u32[]{:S(2)}, u32[]{:S(2)}) collective-permute-start(f32[64,24,128]{2,1,0:T(8,128)S(1)} %get-tuple-element.17), channel_id=1, source_target_pairs={{0,1},{1,0},{2,3},{3,2},{4,5},{5,4},{6,7},{7,6},{8,9},{9,8},{10,11... | collective-permute-start | bytes 2359304 | tf_op jit(solution)/shard_map/ppermute | solution.py:231
  9.8 1.6 %collective-permute-start.1 = (f32[64,8,128]{2,1,0:T(8,128)S(1)}, f32[64,8,128]{2,1,0:T(8,128)S(1)}, u32[]{:S(2)}, u32[]{:S(2)}) collective-permute-start(f32[64,8,128]{2,1,0:T(8,128)S(1)} %get-tuple-element.18), channel_id=1, source_target_pairs={{0,1},{1,0},{2,3},{3,2},{4,5},{5,4},{6,7},{7,6},{8,9},{9,8},{10,11... | collective-permute-start | bytes 786440 | tf_op jit(solution)/shard_map/ppermute | solution.py:231
